TPU v7x, 128 devices: a whole 4x4x4 slice. The times are simulated.
128 devices in a mesh: unit: 16 (over x, y), tm: 8 (over z, core).
Axes of the slice: x: 4, y: 4, z: 4, core: 2. Of those that a mesh axis runs over, the one named last changes fastest.
Arguments:
- spikes: int32 [4096, 16384], P('tm', 'unit'), may hold values from 0 to 2
- stimulus: bfloat16 [4096, 64], P('tm'), may hold values from -6 to 6
- bias: float32 [16384], P('unit'), may hold values from -1.5 to 0
- hist_weight: float32 [10, 16384], P(None, 'unit'), may hold values from -0.9 to 0.9
- stim_filter: bfloat16 [16384, 64], P('unit'), may hold values from -0.5 to 0.5
- coupling_mix: float32 [10], replicated, may hold values from -3 to 3
- coupling_target: int32 [128, 4], P('unit'), may hold values from 0 to 127, as said below
- coupling_weight: bfloat16 [128, 4, 128, 128], P('unit'), may hold values from -0.059814453 to 0.059814453
Outputs:
- grad_bias: float32 [16384], P('unit')
- grad_hist: float32 [10, 16384], P(None, 'unit')
- grad_stim: float32 [16384, 64], P(('unit', 'tm'))
- grad_coupling: float32 [128, 4, 128, 128], P('unit', None, 'tm')
Inputs may be any that keep to these rules, and one draw needn't show every extreme that they name: `coupling_target`: the 4 entries of a row are distinct. Among the rows of one device (8 aligned rows), the targets owned by any one device (tiles k * 8 to k * 8 + 7) are at most 2 distinct tiles, and every owner that is named gets exactly 2.
All inputs are finite; a program needn't handle non-finite values.
Results may differ from a plain program's by a relative error of at most 0.0041.
Values may be sent and summed in bfloat16 or wider, within the bound.
A program may use at most 256 MiB of HBM per device.

v0:
```python
import math

import jax
import jax.numpy as jnp
from jax import lax
from jax.sharding import PartitionSpec as P

TILE = 128
FAN = 4
CAP = 2
NB = 10
LAG = 128


def passed_along(value, axis, steps):
    count = lax.axis_size(axis)
    leading, last = (max(0, -steps), min(count, count - steps))
    return lax.ppermute(value, axis, [(source, source + steps) for source in range(leading, last)])


def raised_cosine(count, lag):
    low = math.log(2.0)
    high = math.log(lag + 1.0)
    spacing = (high - low) / (count - 1)
    stretched = jnp.log(jnp.arange(1, lag + 1).astype(jnp.float32) + 1.0)
    centers = low + spacing * jnp.arange(count).astype(jnp.float32)
    phases = jnp.clip(
        (stretched[None, :] - centers[:, None]) * (math.pi / (2.0 * spacing)), -math.pi, math.pi
    )
    shapes = 0.5 * (1.0 + jnp.cos(phases))
    return (shapes / jnp.sum(shapes, axis=1, keepdims=True)).astype(jnp.bfloat16)


def shards(
    spikes, stimulus, bias, hist_weight, stim_filter, coupling_mix, coupling_target, coupling_weight
):
    time_dev, units_dev = spikes.shape
    tiles_dev = units_dev // TILE
    unit_count = lax.axis_size("unit")
    time_count = lax.axis_size("tm")
    time_total = time_dev * time_count
    block_rows = min(time_dev, 4 * LAG)
    counts_bf = spikes.astype(jnp.bfloat16)
    previous = passed_along(counts_bf[time_dev - LAG :], "tm", 1)
    extended = jnp.concatenate([previous, counts_bf], axis=0)
    basis = raised_cosine(NB, LAG)
    row_index = jnp.arange(block_rows, dtype=jnp.int32)[:, None]
    col_index = jnp.arange(block_rows + LAG, dtype=jnp.int32)[None, :]
    lag_index = LAG + row_index - col_index
    inside = (lag_index >= 1) & (lag_index <= LAG)
    toeplitz = jnp.where(
        inside[None, :, :],
        basis[:, jnp.clip(lag_index - 1, 0, LAG - 1)],
        jnp.zeros((), jnp.bfloat16),
    )
    history_blocks = jnp.einsum(
        "bkw,wu->bku", toeplitz, extended, preferred_element_type=jnp.float32
    )
    mixed = jnp.sum(coupling_mix[:, None, None] * history_blocks, axis=0).astype(jnp.bfloat16)
    mixed_tiles = mixed.reshape(time_dev, tiles_dev, TILE)
    slot_count = unit_count * CAP
    flat_target = coupling_target.reshape(-1)
    entry_count = flat_target.shape[0]
    owner = flat_target // tiles_dev
    local_tile = flat_target % tiles_dev
    entry_index = jnp.arange(entry_count, dtype=jnp.int32)
    same_tile = flat_target[:, None] == flat_target[None, :]
    first_seen = jnp.logical_not(
        jnp.any(same_tile & (entry_index[None, :] < entry_index[:, None]), axis=1)
    )
    lower_rank = (
        (owner[:, None] == owner[None, :])
        & (local_tile[None, :] < local_tile[:, None])
        & first_seen[None, :]
    )
    slot_of = owner * CAP + jnp.sum(lower_rank.astype(jnp.int32), axis=1)
    slot_hit = slot_of[None, :] == jnp.arange(slot_count, dtype=jnp.int32)[:, None]
    slot_ids = jnp.max(jnp.where(slot_hit, local_tile[None, :], -1), axis=1)
    slot_table = slot_hit.reshape(slot_count, tiles_dev, FAN).astype(jnp.bfloat16)
    slot_weight = jnp.einsum(
        "csf,sfkn->cskn", slot_table, coupling_weight, preferred_element_type=jnp.float32
    ).astype(jnp.bfloat16)
    partials = jnp.einsum(
        "tsk,cskn->ctn", mixed_tiles, slot_weight, preferred_element_type=jnp.float32
    ).astype(jnp.bfloat16)
    received, received_ids = (
        lax.all_to_all(
            partials.reshape(unit_count, CAP, time_dev, TILE),
            "unit",
            split_axis=0,
            concat_axis=0,
            tiled=True,
        ),
        lax.all_to_all(
            slot_ids.reshape(unit_count, CAP), "unit", split_axis=0, concat_axis=0, tiled=True
        ),
    )
    flat_ids = received_ids.reshape(-1)
    placing = (flat_ids[None, :] == jnp.arange(tiles_dev, dtype=jnp.int32)[:, None]).astype(
        jnp.bfloat16
    )
    coupling = jnp.einsum(
        "jc,ctn->tjn",
        placing,
        received.reshape(slot_count, time_dev, TILE),
        preferred_element_type=jnp.float32,
    ).reshape(time_dev, units_dev)
    drive = jnp.einsum("tc,uc->tu", stimulus, stim_filter, preferred_element_type=jnp.float32)
    logit = (
        bias[None, :] + drive + jnp.sum(history_blocks * hist_weight[:, None, :], axis=0) + coupling
    )
    resid = spikes.astype(jnp.float32) - jnp.exp(logit)
    resid_bf = resid.astype(jnp.bfloat16)
    bias_total, hist_total = lax.psum(
        (jnp.sum(resid, axis=0), jnp.sum(history_blocks * resid[None, :, :], axis=1)), "tm"
    )
    grad_bias = bias_total / time_total
    grad_hist = hist_total / time_total
    everyone = lax.all_gather(resid_bf, "unit", axis=1, tiled=True)
    picking = (
        flat_target[:, None] == jnp.arange(tiles_dev * unit_count, dtype=jnp.int32)[None, :]
    ).astype(jnp.bfloat16)
    selected = jnp.einsum(
        "ej,tjn->ten",
        picking,
        everyone.reshape(time_dev, tiles_dev * unit_count, TILE),
        preferred_element_type=jnp.float32,
    ).astype(jnp.bfloat16)
    selected = selected.reshape(time_dev, tiles_dev, FAN, TILE)
    coupling_terms = jnp.einsum(
        "tsk,tsfn->sfkn", mixed_tiles, selected, preferred_element_type=jnp.float32
    )
    grad_coupling = (
        lax.psum_scatter(coupling_terms, "tm", scatter_dimension=2, tiled=True) / time_total
    )
    swapped = lax.all_to_all(resid_bf, "tm", split_axis=1, concat_axis=0, tiled=True)
    stim_total = jnp.einsum(
        "tu,tc->uc",
        swapped,
        lax.all_gather(stimulus, "tm", axis=0, tiled=True),
        preferred_element_type=jnp.float32,
    )
    grad_stim = stim_total / time_total
    return (grad_bias, grad_hist, grad_stim, grad_coupling)


def solution(mesh):
    return jax.shard_map(
        shards,
        mesh=mesh,
        in_specs=(
            P("tm", "unit"),
            P("tm", None),
            P("unit"),
            P(None, "unit"),
            P("unit", None),
            P(),
            P("unit", None),
            P("unit", None, None, None),
        ),
        out_specs=(
            P("unit"),
            P(None, "unit"),
            P(("unit", "tm"), None),
            P("unit", None, "tm", None),
        ),
        check_vma=False,
    )
```

profile of v0, /device:TPU:1, one launch (start us, length us, event | category | flops | bytes accessed | tf_op | source)
XLA Modules:
  0.0 1556.0 jit_solution(9174571685299612197)
XLA Ops:
  7.2 1.9 convert_element_type.65
  10.1 4.9 collective-permute-start
  16.5 6.8 all-to-all-start.1
  23.3 1.5 compare_select_fusion
  27.7 5.2 convert_bitcast_fusion
  33.2 1133.5 %gather_fusion = bf16[327680,10]{1,0:T(8,128)(2,1)} fusion(bf16[10,128]{0,1:T(8,128)(2,1)S(1)} %copy.67, s32[327680]{0:T(1024)S(1)} %copy-done.5), kind=kCustom, calls=%fused_computation | custom fusion | bytes 14417920 | tf_op jit(solution)/shard_map/gather | solution.py:53
  1166.6 62.6 %copy.68 = bf16[512,640,10]{1,0,2:T(8,128)(2,1)} copy(bf16[512,640,10]{2,1,0:T(8,128)(2,1)} %bitcast) | data formatting | bytes 13107200 | tf_op jit(solution)/shard_map/gather | solution.py:53
  1229.7 16.5 %multiply_reduce_fusion.2 = (f32[512,1024]{1,0:T(8,128)S(1)}, bf16[512,1024]{1,0:T(8,128)(2,1)}, f32[10,512,1024]{2,1,0:T(8,128)}) fusion(f32[10,1024]{1,0:T(8,128)S(1)} %copy-done.12, f32[10]{0:T(128)S(1)} %copy-done.13, bf16[512,1024]{1,0:T(8,128)(2,1)S(1)} %copy-done.7, bf16[128,1024]{1,0:T(8,128)(2,1)S(1)} %collective-permute-done, ...), kind=kOutput, calls=%fused_computation.3 | convolution fusion | flops 6736707584 | bytes 32350248 | tf_op jit(solution)/shard_map/bkw,wu->bku/dot_general | solution.py:56
  1247.7 22.9 %bitcast_convert_fusion = bf16[32,128,512]{2,1,0:T(8,128)(2,1)} fusion(bf16[512,8,128,1]{0,2,1,3:T(8,128)(2,1)S(1)} %bitcast.77, bf16[32,8,128,128]{3,0,2,1:T(8,128)(2,1)} %convert_bitcast_fusion), kind=kOutput, calls=%fused_computation.4 | convolution fusion | flops 4297064448 | bytes 13631488 | tf_op jit(solution)/shard_map/tsk,cskn->ctn/dot_general | solution.py:83
  1270.5 6.7 all-to-all-start
  1278.6 53.9 %all-to-all-done = bf16[16,2,512,128]{2,3,1,0:T(8,128)(2,1)} async-done(((bf16[16,2,512,128]{2,3,1,0:T(8,128)(2,1)}), bf16[16,2,512,128]{2,3,1,0:T(8,128)(2,1)}, u32[]{:S(2)}, u32[]{:S(2)}) %all-to-all-start) | async-done | bytes 4194336 | tf_op jit(solution)/shard_map/all_to_all | solution.py:87
  1332.5 11.3 copy.78
  1343.8 3.0 fusion.36
  1346.8 2.6 fusion.41
  1349.5 121.8 %all-gather.2.cloned.1.call-done = bf16[512,16384]{1,0:T(8,128)(2,1)} async-done(((bf16[512,1024]{1,0:T(8,128)(2,1)}), bf16[512,16384]{1,0:T(8,128)(2,1)}) %all-gather.2.cloned.1.call-update) | async-done | bytes 16777232 | tf_op jit(solution)/shard_map/all_gather | solution.py:119
  1471.3 9.8 copy.94
  1481.1 2.6 convolution_convert_fusion
  1483.7 2.1 fusion.13
  1485.8 2.1 copy.83
  1487.9 15.4 all_gather.6
  1504.5 4.3 all-to-all-start.2
  1508.8 8.7 multiply_reduce_fusion
  1517.5 26.3 %all-reduce = (f32[1024]{0:T(1024)S(1)}, f32[10,1024]{1,0:T(8,128)S(1)}) all-reduce(f32[1024]{0:T(1024)S(1)} %get-tuple-element.29, f32[10,1024]{1,0:T(8,128)S(1)} %multiply_reduce_fusion), channel_id=1, replica_groups=mesh['unit'=16,'tm'=8] {'tm'}, use_global_device_ids=true, to_apply=%region_7.8 | all-reduce | flops 11264 | bytes 90112 | tf_op jit(solution)/shard_map/psum | solution.py:114
  1545.0 2.3 convolution_multiply_fusion
  (66 shorter events, 13.1 us)
Async XLA Ops:
  7.2 20.5 %copy-start = (bf16[8,4,128,128]{3,2,1,0:T(8,128)(2,1)S(1)}, bf16[8,4,128,128]{3,2,1,0:T(8,128)(2,1)}, u32[]{:S(2)}) copy-start(bf16[8,4,128,128]{3,2,1,0:T(8,128)(2,1)} %param.15) | copy-start | bytes 3145732
  7.2 7.9 copy-start.11
  9.1 1.0 copy-start.6
  10.1 1219.5 %collective-permute-start = (bf16[128,1024]{1,0:T(8,128)(2,1)S(1)}, bf16[128,1024]{1,0:T(8,128)(2,1)S(1)}, u32[]{:S(2)}, u32[]{:S(2)}) collective-permute-start(bf16[128,1024]{1,0:T(8,128)(2,1)S(1)} %slice.6), channel_id=1, source_target_pairs={{0,1},{1,2},{2,3},{3,4},{4,5},{5,6},{6,7},{8,9},{9,10},{10,11},{11... | collective-permute-start | bytes 786440 | tf_op jit(solution)/shard_map/ppermute | solution.py:18
  16.5 1254.1 %all-to-all-start.1 = ((s32[16,1,2]{2,1,0:T(1,128)}), s32[16,1,2]{2,1,0:T(1,128)S(1)}, u32[]{:S(2)}, u32[]{:S(2)}) async-start(s32[16,1,2]{2,1,0:T(1,128)} %bitcast.13), calls=%async_computation.1 | async-start | bytes 16384 | tf_op jit(solution)/shard_map/all_to_all | solution.py:94
  27.7 5.4 copy-start.5
  1166.6 63.0 %copy-start.7 = (bf16[512,1024]{1,0:T(8,128)(2,1)S(1)}, bf16[512,1024]{1,0:T(8,128)(2,1)}, u32[]{:S(2)}) copy-start(bf16[512,1024]{1,0:T(8,128)(2,1)} %copy-done.6) | copy-start | bytes 3145732
  1166.6 63.0 %copy-start.12 = (f32[10,1024]{1,0:T(8,128)S(1)}, f32[10,1024]{1,0:T(8,128)}, u32[]{:S(2)}) copy-start(f32[10,1024]{1,0:T(8,128)} %param.11) | copy-start | bytes 122884
  1166.6 63.0 %copy-start.13 = (f32[10]{0:T(128)S(1)}, f32[10]{0:T(128)}, u32[]{:S(2)}) copy-start(f32[10]{0:T(128)} %param.13) | copy-start | bytes 124
  1270.5 61.9 %all-to-all-start = ((bf16[16,2,512,128]{2,3,1,0:T(8,128)(2,1)}), bf16[16,2,512,128]{2,3,1,0:T(8,128)(2,1)}, u32[]{:S(2)}, u32[]{:S(2)}) async-start(bf16[16,2,512,128]{2,3,1,0:T(8,128)(2,1)} %bitcast.76), calls=%async_computation | async-start | bytes 8388608 | tf_op jit(solution)/shard_map/all_to_all | solution.py:87
  1277.3 194.1 %all-gather.2.cloned.1.call-start = ((), (), s32[]{:S(2)}) async-start(), calls=%async_computation.4 | async-start | bytes 17825792 | tf_op jit(solution)/shard_map/all_gather | solution.py:119
  1343.8 3.0 copy-start.3
  1343.8 3.0 copy-start.8
  1343.8 3.0 copy-start.9
  1343.8 3.0 copy-start.10
  1349.4 197.9 %reduce-scatter.2.cloned.1.call-start = ((), (), s32[]{:S(2)}) async-start(), calls=%async_computation.5 | async-start | bytes 2359296 | tf_op jit(solution)/shard_map/reduce_scatter | solution.py:134
  1487.8 15.5 copy-start.2
  1503.3 5.5 copy-start.4
  1504.5 40.6 %all-to-all-start.2 = ((bf16[512,8,128]{2,0,1:T(8,128)(2,1)}), bf16[512,8,128]{2,0,1:T(8,128)(2,1)}, u32[]{:S(2)}, u32[]{:S(2)}) async-start(bf16[512,8,128]{2,0,1:T(8,128)(2,1)} %copy_bitcast_fusion), calls=%async_computation.2 | async-start | bytes 2097152 | tf_op jit(solution)/shard_map/all_to_all | solution.py:136
  1508.7 40.5 %copy-start.1 = (bf16[8,4,128,128]{3,2,1,0:T(8,128)(2,1)S(1)}, bf16[8,4,128,128]{3,2,1,0:T(8,128)(2,1)}, u32[]{:S(2)}) copy-start(bf16[8,4,128,128]{3,2,1,0:T(8,128)(2,1)} %param.15) | copy-start | bytes 3145732
Sparse Core Ops, SparseCore 0:
  1349.6 121.7 all-gather.1
  1488.0 37.2 reduce-scatter.1
where the time goes:
time: 1560 us
  local copies, waits for them, and re-layouts  1230 us (79%)
  waiting for transfers between devices  176 us (11%)
  matrix products  57.1 us (4%)
  blocking collectives  41.7 us (3%)
  starting transfers between devices  22.8 us (1%)
  other arithmetic  17.5 us (1%)
    gather x2, local copies, waits for them, and re-layouts, shards(): basis[:, jnp.clip(lag_index - 1, 0, LAG - 1)]  1200 us
    all_gather x1, waiting for transfers between devices, shards(): everyone = lax.all_gather(resid_bf, 'unit', axis=1, tiled=True)  122 us
    all_to_all x1, waiting for transfers between devices, shards(): lax.all_to_all(partials.reshape(unit_count, CAP, time_dev, TILE), 'unit',...  53.9 us
  transfers between devices with their start and end apart: 6, of which 2 were waited for; matrix products, arithmetic and copies ran while one was open for 81% of the time, Pallas kernels for 0%

commit v1 on v0

--- a/solution.py
+++ b/solution.py
@@ -39,23 +39,17 @@
     unit_count = lax.axis_size("unit")
     time_count = lax.axis_size("tm")
     time_total = time_dev * time_count
-    block_rows = min(time_dev, 4 * LAG)
+    blocks = time_dev // LAG
     counts_bf = spikes.astype(jnp.bfloat16)
     previous = passed_along(counts_bf[time_dev - LAG :], "tm", 1)
     extended = jnp.concatenate([previous, counts_bf], axis=0)
     basis = raised_cosine(NB, LAG)
-    row_index = jnp.arange(block_rows, dtype=jnp.int32)[:, None]
-    col_index = jnp.arange(block_rows + LAG, dtype=jnp.int32)[None, :]
-    lag_index = LAG + row_index - col_index
-    inside = (lag_index >= 1) & (lag_index <= LAG)
-    toeplitz = jnp.where(
-        inside[None, :, :],
-        basis[:, jnp.clip(lag_index - 1, 0, LAG - 1)],
-        jnp.zeros((), jnp.bfloat16),
-    )
+    period = jnp.concatenate([basis[:, ::-1], jnp.zeros((NB, LAG + 1), jnp.bfloat16)], axis=1)
+    toeplitz = jnp.tile(period, (1, LAG))[:, : 2 * LAG * LAG].reshape(NB, LAG, 2 * LAG)
+    windows = jnp.stack([extended[w * LAG : (w + 2) * LAG] for w in range(blocks)])
     history_blocks = jnp.einsum(
-        "bkw,wu->bku", toeplitz, extended, preferred_element_type=jnp.float32
-    )
+        "brc,wcu->bwru", toeplitz, windows, preferred_element_type=jnp.float32
+    ).reshape(NB, time_dev, units_dev)
     mixed = jnp.sum(coupling_mix[:, None, None] * history_blocks, axis=0).astype(jnp.bfloat16)
     mixed_tiles = mixed.reshape(time_dev, tiles_dev, TILE)
     slot_count = unit_count * CAP
@@ -116,31 +110,28 @@
     )
     grad_bias = bias_total / time_total
     grad_hist = hist_total / time_total
-    everyone = lax.all_gather(resid_bf, "unit", axis=1, tiled=True)
-    picking = (
-        flat_target[:, None] == jnp.arange(tiles_dev * unit_count, dtype=jnp.int32)[None, :]
+    resid_tiles = resid_bf.reshape(time_dev, tiles_dev, TILE).transpose(1, 0, 2)
+    outgoing = jnp.einsum(
+        "jc,jtn->ctn", placing, resid_tiles, preferred_element_type=jnp.float32
     ).astype(jnp.bfloat16)
+    slots = lax.all_to_all(
+        outgoing.reshape(unit_count, CAP, time_dev, TILE),
+        "unit",
+        split_axis=0,
+        concat_axis=0,
+        tiled=True,
+    ).reshape(slot_count, time_dev, TILE)
     selected = jnp.einsum(
-        "ej,tjn->ten",
-        picking,
-        everyone.reshape(time_dev, tiles_dev * unit_count, TILE),
-        preferred_element_type=jnp.float32,
-    ).astype(jnp.bfloat16)
-    selected = selected.reshape(time_dev, tiles_dev, FAN, TILE)
+        "ce,ctn->etn", slot_hit.astype(jnp.bfloat16), slots, preferred_element_type=jnp.float32
+    ).astype(jnp.bfloat16).reshape(tiles_dev, FAN, time_dev, TILE)
     coupling_terms = jnp.einsum(
-        "tsk,tsfn->sfkn", mixed_tiles, selected, preferred_element_type=jnp.float32
+        "tsk,sftn->sfkn", mixed_tiles, selected, preferred_element_type=jnp.float32
     )
     grad_coupling = (
         lax.psum_scatter(coupling_terms, "tm", scatter_dimension=2, tiled=True) / time_total
     )
-    swapped = lax.all_to_all(resid_bf, "tm", split_axis=1, concat_axis=0, tiled=True)
-    stim_total = jnp.einsum(
-        "tu,tc->uc",
-        swapped,
-        lax.all_gather(stimulus, "tm", axis=0, tiled=True),
-        preferred_element_type=jnp.float32,
-    )
-    grad_stim = stim_total / time_total
+    stim_terms = jnp.einsum("tu,tc->uc", resid_bf, stimulus, preferred_element_type=jnp.float32)
+    grad_stim = lax.psum_scatter(stim_terms, "tm", scatter_dimension=0, tiled=True) / time_total
     return (grad_bias, grad_hist, grad_stim, grad_coupling)
 
 

time: 1560 us -> 289 us (0.19)
  local copies, waits for them, and re-layouts: 1230 us -> 39.7 us
  waiting for transfers between devices: 176 us -> 113 us
  blocking collectives: 41.7 us -> 21.7 us
    gather x2 -> x0, local copies, waits for them, and re-layouts: 1200 us -> none  [shards(): basis[:, jnp.clip(lag_index - 1, 0, LAG - 1)]]
    all_gather x1 -> x0, waiting for transfers between devices: 122 us -> none  [shards(): everyone = lax.all_gather(resid_bf, 'unit', axis=1, tiled=True)]
    all_to_all x1, waiting for transfers between devices: 0.01 us -> 55.1 us  [shards(): lax.all_to_all(outgoing.reshape(unit_count, CAP, time_dev, TILE), 'unit',...]
  transfers between devices with their start and end apart: 6 -> 6, of which waited for: 2 -> 3; matrix products, arithmetic and copies ran while one was open for 81% -> 24% of each run, Pallas kernels for 0% -> 0%
where the time goes in v1:
time: 289 us; the launch traced here: 284 us
  waiting for transfers between devices  113 us (39%)
  matrix products  43.8 us (15%)
  local copies, waits for them, and re-layouts  39.7 us (14%)
  starting transfers between devices  35.4 us (12%)
  blocking collectives  21.7 us (8%)
  other arithmetic  16 us (6%)
  between operations  14.3 us (5%)
    all_to_all x1, waiting for transfers between devices, shards(): lax.all_to_all(outgoing.reshape(unit_count, CAP, time_dev, TILE), 'unit',...  55.1 us
    all_to_all x1, waiting for transfers between devices, shards(): lax.all_to_all(partials.reshape(unit_count, CAP, time_dev, TILE), 'unit',...  52.3 us
    psum x1, blocking collectives, shards(): lax.psum((jnp.sum(resid, axis=0), jnp.sum(history_blocks * resid[None, :,...  21.7 us
    all_to_all x1, starting transfers between devices, shards(): lax.all_to_all(outgoing.reshape(unit_count, CAP, time_dev, TILE), 'unit',...  16.2 us
    dot_general x1, matrix products, shards(): jnp.einsum('tsk,cskn->ctn', mixed_tiles, slot_weight, preferred_element_t...  13.8 us
    dot_general x1, matrix products, shards(): jnp.einsum('brc,wcu->bwru', toeplitz, windows, preferred_element_type=jnp...  11.5 us
    all_to_all x1, local copies, waits for them, and re-layouts, shards(): lax.all_to_all(partials.reshape(unit_count, CAP, time_dev, TILE), 'unit',...  11.3 us
    reduce_sum x1, other arithmetic, shards(): jnp.sum(history_blocks * resid[None, :, :], axis=1)  8.63 us
  transfers between devices with their start and end apart: 6, of which 3 were waited for; matrix products, arithmetic and copies ran while one was open for 24% of the time, Pallas kernels for 0%

profile of v1, /device:TPU:1, one launch (start us, length us, event | category | flops | bytes accessed | tf_op | source)
XLA Modules:
  0.0 284.4 jit_solution(1496224668683497769)
XLA Ops:
  9.2 7.6 %all-to-all-start.1 = ((s32[16,1,2]{2,1,0:T(1,128)}), s32[16,1,2]{2,1,0:T(1,128)S(1)}, u32[]{:S(2)}, u32[]{:S(2)}) async-start(s32[16,1,2]{2,1,0:T(1,128)} %bitcast.17), calls=%async_computation.1 | async-start | bytes 16384 | tf_op jit(solution)/shard_map/all_to_all | solution.py:88
  16.8 1.8 convert_element_type.62
  19.4 4.4 %collective-permute-start = (bf16[128,1024]{1,0:T(8,128)(2,1)}, bf16[128,1024]{1,0:T(8,128)(2,1)S(1)}, u32[]{:S(2)}, u32[]{:S(2)}) collective-permute-start(bf16[128,1024]{1,0:T(8,128)(2,1)} %slice.24), channel_id=1, source_target_pairs={{0,1},{1,2},{2,3},{3,4},{4,5},{5,6},{6,7},{8,9},{9,10},{10,11},{11... | collective-permute-start | bytes 786440 | tf_op jit(solution)/shard_map/ppermute | solution.py:18
  24.3 1.0 tile.4
  25.4 3.2 %tile.10 = bf16[10,32896]{1,0:T(8,128)(2,1)S(1)} reshape(bf16[10,128,257]{2,1,0:T(8,128)(2,1)} %tile.4) | data formatting | bytes 1315840 | tf_op jit(solution)/shard_map/tile | solution.py:48
  28.9 3.3 %convert_bitcast_fusion = bf16[32,8,128,128]{3,0,2,1:T(8,128)(2,1)S(1)} fusion(bf16[8,4,128,128]{3,2,1,0:T(8,128)(2,1)S(1)} %copy-done, s32[8,4]{1,0:T(8,128)S(1)} %fusion.42), kind=kOutput, calls=%fused_computation.9 | convolution fusion | flops 37749760 | bytes 9437312 | tf_op jit(solution)/shard_map/csf,sfkn->cskn/dot_general | solution.py:74
  33.1 11.5 %fusion = (f32[4,128,1024]{2,1,0:T(8,128)}, bf16[4,128,1024]{2,1,0:T(8,128)(2,1)S(1)}, f32[4,1024,10,128]{1,3,2,0:T(8,128)}) fusion(f32[10,1024]{1,0:T(8,128)S(1)} %copy-done.9, f32[10]{0:T(128)S(1)} %copy-done.10, bf16[16,128,256]{2,1,0:T(8,128)(2,1)S(1)} %bitcast.104, bf16[1,256,1024]{2,1,0:T(8,128)(2,1)S(1)} %get-tuple-element.27, ...), kind=kOutput, calls=%fused_computation.3 | convolution fusion | flops 2712666112 | bytes 26935808 | tf_op jit(solution)/shard_map/brc,wcu->bwru/dot_general | solution.py:50
  44.9 13.8 %bitcast_convert_fusion = bf16[32,128,512]{2,1,0:T(8,128)(2,1)} fusion(bf16[32,8,128,128]{3,0,2,1:T(8,128)(2,1)S(1)} %convert_bitcast_fusion, bf16[512,8,128]{2,1,0:T(8,128)(2,1)S(1)} %bitcast.102), kind=kOutput, calls=%fused_computation.6 | convolution fusion | flops 4297064448 | bytes 13631488 | tf_op jit(solution)/shard_map/tsk,cskn->ctn/dot_general | solution.py:77
  58.7 7.0 %all-to-all-start = ((bf16[16,2,512,128]{2,3,1,0:T(8,128)(2,1)}), bf16[16,2,512,128]{2,3,1,0:T(8,128)(2,1)}, u32[]{:S(2)}, u32[]{:S(2)}) async-start(bf16[16,2,512,128]{2,3,1,0:T(8,128)(2,1)} %bitcast.98), calls=%async_computation | async-start | bytes 8388608 | tf_op jit(solution)/shard_map/all_to_all | solution.py:81
  67.0 52.3 %all-to-all-done = bf16[16,2,512,128]{2,3,1,0:T(8,128)(2,1)} async-done(((bf16[16,2,512,128]{2,3,1,0:T(8,128)(2,1)}), bf16[16,2,512,128]{2,3,1,0:T(8,128)(2,1)}, u32[]{:S(2)}, u32[]{:S(2)}) %all-to-all-start) | async-done | bytes 4194336 | tf_op jit(solution)/shard_map/all_to_all | solution.py:81
  119.3 11.3 %copy.54 = bf16[16,2,512,128]{3,1,0,2:T(2,128)(2,1)} copy(bf16[16,2,512,128]{2,3,1,0:T(8,128)(2,1)} %all-to-all-done) | data formatting | bytes 8388608 | tf_op jit(solution)/shard_map/all_to_all | solution.py:81
  130.6 3.0 %fusion.46 = f32[512,128,8]{1,2,0:T(8,128)S(1)} fusion(bf16[32,512,128]{2,0,1:T(8,128)(2,1)} %bitcast.96, s32[32]{0:T(128)S(1)} %eq.69), kind=kOutput, calls=%fused_computation.70 | convolution fusion | flops 33554688 | bytes 6291584 | tf_op jit(solution)/shard_map/jc,ctn->tjn/dot_general | solution.py:96
  135.6 3.3 %convolution_convert_fusion = bf16[32,512,128]{2,0,1:T(8,128)(2,1)} fusion(bf16[512,8,128]{2,1,0:T(8,128)(2,1)S(1)} %bitcast.101, s32[32]{0:T(128)S(1)} %eq.69), kind=kOutput, calls=%fused_computation.12 | convolution fusion | flops 35651840 | bytes 5243008 | tf_op jit(solution)/shard_map/jc,jtn->ctn/dot_general | solution.py:114
  138.9 8.0 %copy.56 = bf16[16,2,512,128]{3,1,2,0:T(2,128)(2,1)} copy(bf16[16,2,512,128]{3,1,0,2:T(2,128)(2,1)} %bitcast.94) | data formatting | bytes 8388608 | tf_op jit(solution)/shard_map/reshape | solution.py:118
  146.9 16.2 %all-to-all-start.2 = ((bf16[16,2,512,128]{3,1,2,0:T(2,128)(2,1)}), bf16[16,2,512,128]{3,1,2,0:T(2,128)(2,1)}, u32[]{:S(2)}, u32[]{:S(2)}) async-start(bf16[16,2,512,128]{3,1,2,0:T(2,128)(2,1)} %copy.56), calls=%async_computation.3 | async-start | bytes 8388608 | tf_op jit(solution)/shard_map/all_to_all | solution.py:117
  164.4 55.1 %all-to-all-done.2 = bf16[16,2,512,128]{3,1,2,0:T(2,128)(2,1)} async-done(((bf16[16,2,512,128]{3,1,2,0:T(2,128)(2,1)}), bf16[16,2,512,128]{3,1,2,0:T(2,128)(2,1)}, u32[]{:S(2)}, u32[]{:S(2)}) %all-to-all-start.2) | async-done | bytes 4194336 | tf_op jit(solution)/shard_map/all_to_all | solution.py:117
  219.5 7.0 %copy.57 = bf16[16,2,512,128]{3,1,0,2:T(2,128)(2,1)} copy(bf16[16,2,512,128]{3,1,2,0:T(2,128)(2,1)} %all-to-all-done.2) | data formatting | bytes 8388608 | tf_op jit(solution)/shard_map/all_to_all | solution.py:117
  226.6 3.6 %convolution_convert_fusion.1 = bf16[32,512,128]{2,0,1:T(8,128)(2,1)S(1)} fusion(bf16[32,512,128]{2,0,1:T(8,128)(2,1)} %bitcast.95, s32[32]{0:T(128)S(1)} %multiply_add_fusion), kind=kOutput, calls=%fused_computation.13 | convolution fusion | flops 136315904 | bytes 8388736 | tf_op jit(solution)/shard_map/ce,ctn->etn/dot_general | solution.py:124
  230.2 3.5 %fusion.18 = f32[8,4,128,128]{2,3,1,0:T(8,128)} fusion(bf16[8,4,512,128]{3,1,0,2:T(4,128)(2,1)S(1)} %bitcast.99, bf16[512,8,128,1]{2,1,0,3:T(8,128)(2,1)S(1)} %bitcast.103), kind=kOutput, calls=%fused_computation.26 | convolution fusion | flops 536870912 | bytes 7340032 | tf_op jit(solution)/shard_map/tsk,sftn->sfkn/dot_general | solution.py:127
  233.6 3.1 %copy.60 = f32[8,4,128,128]{3,0,1,2:T(8,128)} copy(f32[8,4,128,128]{2,3,1,0:T(8,128)} %fusion.18) | data formatting | bytes 4194304 | tf_op jit(solution)/shard_map/tsk,sftn->sfkn/transpose | solution.py:127
  236.8 8.6 %fusion.2 = f32[10,1024]{1,0:T(8,128)S(1)} fusion(f32[4,1024,10,128]{1,3,2,0:T(8,128)} %get-tuple-element.32, f32[4,128,1024]{2,1,0:T(8,128)S(1)} %bitcast.93), kind=kLoop, calls=%fused_computation.5 | loop fusion | flops 10475520 | bytes 23109632 | tf_op jit(solution)/shard_map/reduce_sum | solution.py:109
  245.4 21.7 %all-reduce.1 = (f32[1024]{0:T(1024)S(1)}, f32[10,1024]{1,0:T(8,128)S(1)}) all-reduce(f32[1024]{0:T(1024)S(1)} %get-tuple-element.25, f32[10,1024]{1,0:T(8,128)S(1)} %fusion.2), channel_id=1, replica_groups=mesh['unit'=16,'tm'=8] {'tm'}, use_global_device_ids=true, to_apply=%region_7.8 | all-reduce | flops 11264 | bytes 90112 | tf_op jit(solution)/shard_map/psum | solution.py:108
  268.4 1.4 broadcast_multiply_fusion.2
  269.8 5.9 %reduce-scatter.5.cloned.1.call-done = f32[8,4,16,128]{3,0,1,2:T(8,128)} async-done(((f32[8,4,128,128]{3,0,1,2:T(8,128)}), f32[8,4,16,128]{3,0,1,2:T(8,128)}) %reduce-scatter.5.cloned.1.call-update) | async-done | bytes 262160 | tf_op jit(solution)/shard_map/reduce_scatter | solution.py:131
  (62 shorter events, 12.3 us)
Async XLA Ops:
  7.2 21.8 %copy-start = (bf16[8,4,128,128]{3,2,1,0:T(8,128)(2,1)S(1)}, bf16[8,4,128,128]{3,2,1,0:T(8,128)(2,1)}, u32[]{:S(2)}) copy-start(bf16[8,4,128,128]{3,2,1,0:T(8,128)(2,1)} %param.15) | copy-start | bytes 3145732
  9.2 49.4 %all-to-all-start.1 = ((s32[16,1,2]{2,1,0:T(1,128)}), s32[16,1,2]{2,1,0:T(1,128)S(1)}, u32[]{:S(2)}, u32[]{:S(2)}) async-start(s32[16,1,2]{2,1,0:T(1,128)} %bitcast.17), calls=%async_computation.1 | async-start | bytes 16384 | tf_op jit(solution)/shard_map/all_to_all | solution.py:88
  19.4 12.9 %collective-permute-start = (bf16[128,1024]{1,0:T(8,128)(2,1)}, bf16[128,1024]{1,0:T(8,128)(2,1)S(1)}, u32[]{:S(2)}, u32[]{:S(2)}) collective-permute-start(bf16[128,1024]{1,0:T(8,128)(2,1)} %slice.24), channel_id=1, source_target_pairs={{0,1},{1,2},{2,3},{3,4},{4,5},{5,6},{6,7},{8,9},{9,10},{10,11},{11... | collective-permute-start | bytes 786440 | tf_op jit(solution)/shard_map/ppermute | solution.py:18
  32.2 0.8 copy-start.9
  32.2 0.8 copy-start.10
  44.9 13.8 %copy-start.4 = (bf16[64,8,8,128]{3,2,1,0:T(8,128)(2,1)}, bf16[64,8,8,128]{3,2,1,0:T(8,128)(2,1)S(1)}, u32[]{:S(2)}) copy-start(bf16[64,8,8,128]{3,2,1,0:T(8,128)(2,1)S(1)} %copy.69) | copy-start | bytes 3145732
  58.7 60.6 %all-to-all-start = ((bf16[16,2,512,128]{2,3,1,0:T(8,128)(2,1)}), bf16[16,2,512,128]{2,3,1,0:T(8,128)(2,1)}, u32[]{:S(2)}, u32[]{:S(2)}) async-start(bf16[16,2,512,128]{2,3,1,0:T(8,128)(2,1)} %bitcast.98), calls=%async_computation | async-start | bytes 8388608 | tf_op jit(solution)/shard_map/all_to_all | solution.py:81
  130.6 3.0 %copy-start.2 = (s32[512,1024]{1,0:T(8,128)S(1)}, s32[512,1024]{1,0:T(8,128)}, u32[]{:S(2)}) copy-start(s32[512,1024]{1,0:T(8,128)} %param.8) | copy-start | bytes 6291460
  130.6 3.5 %copy-start.3 = (f32[4,128,1024]{2,1,0:T(8,128)S(1)}, f32[4,128,1024]{2,1,0:T(8,128)}, u32[]{:S(2)}) copy-start(f32[4,128,1024]{2,1,0:T(8,128)} %get-tuple-element.20) | copy-start | bytes 6291460
  130.6 3.5 %copy-start.6 = (bf16[512,64]{0,1:T(8,128)(2,1)S(1)}, bf16[512,64]{0,1:T(8,128)(2,1)}, u32[]{:S(2)}) copy-start(bf16[512,64]{0,1:T(8,128)(2,1)} %param.9) | copy-start | bytes 196612
  130.6 3.5 %copy-start.7 = (bf16[1024,64]{0,1:T(8,128)(2,1)S(1)}, bf16[1024,64]{0,1:T(8,128)(2,1)}, u32[]{:S(2)}) copy-start(bf16[1024,64]{0,1:T(8,128)(2,1)} %param.12) | copy-start | bytes 393220
  130.6 3.5 %copy-start.8 = (f32[1024]{0:T(1024)S(1)}, f32[1024]{0:T(1024)}, u32[]{:S(2)}) copy-start(f32[1024]{0:T(1024)} %param.10) | copy-start | bytes 12292
  146.9 72.7 %all-to-all-start.2 = ((bf16[16,2,512,128]{3,1,2,0:T(2,128)(2,1)}), bf16[16,2,512,128]{3,1,2,0:T(2,128)(2,1)}, u32[]{:S(2)}, u32[]{:S(2)}) async-start(bf16[16,2,512,128]{3,1,2,0:T(2,128)(2,1)} %copy.56), calls=%async_computation.3 | async-start | bytes 8388608 | tf_op jit(solution)/shard_map/all_to_all | solution.py:117
  163.1 105.3 %reduce-scatter.3.cloned.1.call-start = ((), (), s32[]{:S(2)}) async-start(), calls=%async_computation.5 | async-start | bytes 294912 | tf_op jit(solution)/shard_map/reduce_scatter | solution.py:134
  164.1 111.6 %reduce-scatter.5.cloned.1.call-start = ((), (), s32[]{:S(2)}) async-start(), calls=%async_computation.6 | async-start | bytes 2359296 | tf_op jit(solution)/shard_map/reduce_scatter | solution.py:131
  226.6 3.6 %copy-start.5 = (bf16[64,8,8,128]{3,2,1,0:T(8,128)(2,1)S(1)}, bf16[64,8,8,128]{3,2,1,0:T(8,128)(2,1)}, u32[]{:S(2)}) copy-start(bf16[64,8,8,128]{3,2,1,0:T(8,128)(2,1)} %copy-done.4) | copy-start | bytes 3145732
  236.8 40.7 %copy-start.1 = (bf16[8,4,128,128]{3,2,1,0:T(8,128)(2,1)S(1)}, bf16[8,4,128,128]{3,2,1,0:T(8,128)(2,1)}, u32[]{:S(2)}) copy-start(bf16[8,4,128,128]{3,2,1,0:T(8,128)(2,1)} %param.15) | copy-start | bytes 3145732
Sparse Core Ops, SparseCore 0:
  166.8 29.5 reduce-scatter.2
  236.9 38.7 reduce-scatter.4

commit v2 on v1

v2 whole, which is shorter than its diff:
```python
import functools
import math

import jax
import jax.numpy as jnp
import ml_dtypes
import numpy as np
from jax import lax
from jax.experimental import pallas as pl
from jax.experimental.pallas import tpu as pltpu
from jax.sharding import PartitionSpec as P

TILE = 128
FAN = 4
CAP = 2
NB = 10
LAG = 128
SIDE = 4
PEERS = SIDE * SIDE
SLOTS = PEERS * CAP
TILES_DEV = 8
UNITS_DEV = TILES_DEV * TILE
TIME_DEV = 512
CHUNKS = TIME_DEV // LAG
STIM = 64
TM = 8
WIDE = 2 * TILE
ENTRIES = TILES_DEV * FAN
MESH = pl.DeviceIdType.MESH
F32 = jnp.float32
BF16 = jnp.bfloat16


def toeplitz_table():
    low = math.log(2.0)
    spacing = (math.log(LAG + 1.0) - low) / (NB - 1)
    stretched = np.log(np.arange(1, LAG + 1) + 1.0)
    centers = low + spacing * np.arange(NB)
    phases = (stretched[None, :] - centers[:, None]) * (math.pi / (2.0 * spacing))
    shapes = 0.5 * (1.0 + np.cos(np.clip(phases, -math.pi, math.pi)))
    basis = (shapes / shapes.sum(axis=1, keepdims=True)).astype(np.float32)
    table = np.zeros((NB, LAG, 2 * LAG), np.float32)
    for row in range(LAG):
        table[:, row, row : row + LAG] = basis[:, ::-1]
    return table.reshape(NB * LAG, 2 * LAG).astype(ml_dtypes.bfloat16)


def plan_kernel(target, named, weight_at, slot_at):
    unit = lax.axis_index("unit")
    here_x, here_y = unit // SIDE, unit % SIDE

    @pl.loop(0, PEERS)
    def _(owner):
        named[owner * CAP] = TILES_DEV
        named[owner * CAP + 1] = -1

    @pl.loop(0, SLOTS * TILES_DEV)
    def _(place):
        weight_at[place] = ENTRIES

    @pl.loop(0, ENTRIES)
    def _(entry):
        tile = target[entry // FAN, entry % FAN]
        at = (tile // TILES_DEV) * CAP
        local = tile % TILES_DEV
        named[at] = jnp.minimum(named[at], local)
        named[at + 1] = jnp.maximum(named[at + 1], local)

    @pl.loop(0, ENTRIES)
    def _(entry):
        tile = target[entry // FAN, entry % FAN]
        owner = tile // TILES_DEV
        local = tile % TILES_DEV
        rank = (local == named[owner * CAP + 1]).astype(jnp.int32)
        step_x = lax.rem(owner // SIDE - here_x + SIDE, SIDE)
        step_y = lax.rem(owner % SIDE - here_y + SIDE, SIDE)
        slot = (step_x * SIDE + step_y) * CAP + rank
        slot_at[entry] = slot
        weight_at[slot * TILES_DEV + entry // FAN] = entry


def main_kernel(
    named,
    weight_at,
    slot_at,
    mix,
    spikes,
    stim,
    bias,
    hist_weight,
    filt,
    weights_hbm,
    toeplitz,
    out_bias,
    out_hist,
    out_stim,
    out_coupling,
    ext,
    halo,
    weights,
    hist,
    mixed,
    base,
    partial_out,
    partial_in,
    stage,
    resid_tiles,
    resid_rows,
    resid_out,
    resid_in,
    names,
    grad,
    stats,
    stats_in,
    stim_sum,
    stim_in,
    pair_in,
    pair_out,
    zed_in,
    sem_weights,
    sem_halo,
    sem_names,
    sem_a_send,
    sem_a_recv,
    sem_b_send,
    sem_b_recv,
    sem_stats_send,
    sem_stats_recv,
    sem_stim_send,
    sem_stim_recv,
    sem_pair,
    sem_zed,
):
    unit = lax.axis_index("unit")
    tm = lax.axis_index("tm")
    here_x, here_y = unit // SIDE, unit % SIDE
    here_z, core = tm // 2, tm % 2

    def ahead(step):
        return lax.rem(here_x + step // SIDE, SIDE) * SIDE + lax.rem(here_y + step % SIDE, SIDE)

    def behind(step):
        return lax.rem(here_x - step // SIDE + SIDE, SIDE) * SIDE + lax.rem(
            here_y - step % SIDE + SIDE, SIDE
        )

    def offset(turn):
        step = lax.rem(turn * 5, PEERS)
        step_x, step_y = step // SIDE, step % SIDE
        step_x = lax.rem(step_x + core * (SIDE - step_x + SIDE - step_x), SIDE)
        step_y = lax.rem(step_y + core * (SIDE - step_y + SIDE - step_y), SIDE)
        return step_x * SIDE + step_y

    def around(step):
        return lax.rem(tm + step, TM)

    barrier = pltpu.get_barrier_semaphore()

    @pl.loop(1, PEERS)
    def _(step):
        pl.semaphore_signal(barrier, inc=1, device_id=(ahead(step), tm), device_id_type=MESH)

    @pl.loop(1, TM)
    def _(step):
        pl.semaphore_signal(barrier, inc=1, device_id=(unit, around(step)), device_id_type=MESH)

    weights_copy = pltpu.make_async_copy(
        weights_hbm, weights.at[pl.ds(0, ENTRIES)], sem_weights.at[0]
    )
    weights_copy.start()
    weights[ENTRIES] = jnp.zeros((TILE, TILE), BF16)
    stage[SLOTS] = jnp.zeros((TILE, TILE), BF16)
    stats[...] = jnp.zeros_like(stats)
    stim_sum[...] = jnp.zeros_like(stim_sum)

    @pl.loop(0, CHUNKS)
    def _(chunk):
        rows = pl.ds(pl.multiple_of(chunk * LAG, LAG), LAG)
        later = pl.ds(pl.multiple_of(chunk * LAG + LAG, LAG), LAG)
        ext[later, :] = spikes[rows, :].astype(BF16)

    pl.semaphore_wait(barrier, PEERS - 1 + TM - 1)

    halo_copy = pltpu.make_async_remote_copy(
        src_ref=ext.at[pl.ds(TIME_DEV, LAG)],
        dst_ref=halo,
        send_sem=sem_halo.at[0],
        recv_sem=sem_halo.at[1],
        device_id=(unit, around(1)),
        device_id_type=MESH,
    )
    halo_copy.start()

    def names_copy(step):
        return pltpu.make_async_remote_copy(
            src_ref=named,
            dst_ref=names.at[step],
            send_sem=sem_names.at[0, step],
            recv_sem=sem_names.at[1, step],
            device_id=(ahead(step), tm),
            device_id_type=MESH,
        )

    @pl.loop(1, PEERS)
    def _(step):
        names_copy(step).start()

    def partial_copy(chunk, step):
        pair = pl.ds(step * CAP, CAP)
        return pltpu.make_async_remote_copy(
            src_ref=partial_out.at[chunk, pair],
            dst_ref=partial_in.at[chunk, pair],
            send_sem=sem_a_send.at[chunk, step],
            recv_sem=sem_a_recv.at[chunk, step],
            device_id=(ahead(step), tm),
            device_id_type=MESH,
        )

    def resid_copy(chunk, step):
        pair = pl.ds(step * CAP, CAP)
        return pltpu.make_async_remote_copy(
            src_ref=resid_out.at[chunk, pair],
            dst_ref=resid_in.at[chunk, pair],
            send_sem=sem_b_send.at[chunk, step],
            recv_sem=sem_b_recv.at[chunk, step],
            device_id=(behind(step), tm),
            device_id_type=MESH,
        )

    weights_copy.wait()

    @pl.loop(0, CHUNKS)
    def _(turn):
        chunk = lax.rem(turn + 1, CHUNKS)
        start = pl.multiple_of(chunk * LAG, LAG)
        rows = pl.ds(start, LAG)

        @pl.when(turn == CHUNKS - 1)
        def _():
            halo_copy.wait()
            ext[pl.ds(0, LAG), :] = halo[...] * jnp.minimum(tm, 1).astype(BF16)

        @pl.loop(0, UNITS_DEV // WIDE)
        def _(part):
            left = pl.multiple_of(part * WIDE, WIDE)
            wide = pl.ds(left, WIDE)
            hist[...] = jnp.dot(
                toeplitz[...], ext[pl.ds(start, 2 * LAG), wide], preferred_element_type=F32
            )
            drive = bias[:, wide] + lax.dot_general(
                stim[rows, :],
                filt[wide, :],
                (((1,), (1,)), ((), ())),
                preferred_element_type=F32,
            )
            for half in range(2):
                inner = slice(half * TILE, (half + 1) * TILE)
                cols = pl.ds(pl.multiple_of(left + half * TILE, TILE), TILE)
                blend = jnp.zeros((LAG, TILE), F32)
                own = drive[:, inner]
                for b in range(NB):
                    h = hist[b * LAG : (b + 1) * LAG, inner]
                    blend = blend + mix[b] * h
                    own = own + hist_weight[b : b + 1, cols] * h
                mixed[rows, cols] = blend.astype(BF16)
                base[rows, cols] = own

        @pl.loop(1, PEERS + 1)
        def _(visit):
            step = offset(visit)
            total = jnp.zeros((LAG, WIDE), F32)
            for s in range(0, TILES_DEV, 2):
                at = step * (CAP * TILES_DEV) + s
                top = jnp.concatenate(
                    [weights[weight_at[at]], weights[weight_at[at + TILES_DEV]]], axis=1
                )
                low = jnp.concatenate(
                    [weights[weight_at[at + 1]], weights[weight_at[at + TILES_DEV + 1]]], axis=1
                )
                total = total + jnp.dot(
                    mixed[rows, s * TILE : (s + 2) * TILE],
                    jnp.concatenate([top, low], axis=0),
                    preferred_element_type=F32,
                )
            partial_out[chunk, step * CAP] = total[:, :TILE].astype(BF16)
            partial_out[chunk, step * CAP + 1] = total[:, TILE:].astype(BF16)

            @pl.when(step > 0)
            def _():
                partial_copy(chunk, step).start()

    @pl.loop(1, PEERS)
    def _(step):
        names_copy(step).wait()

    for k in range(CAP * PEERS):
        names[0, k] = named[k]

    @pl.loop(0, CHUNKS)
    def _(turn):
        chunk = lax.rem(turn + 1, CHUNKS)
        start = pl.multiple_of(chunk * LAG, LAG)
        rows = pl.ds(start, LAG)
        spike_rows = pl.ds(pl.multiple_of(start + LAG, LAG), LAG)

        for k in range(CAP):
            stage[k] = partial_out[chunk, k]

        @pl.loop(1, PEERS)
        def _(step):
            partial_copy(chunk, step).wait_recv()
            for k in range(CAP):
                stage[step * CAP + k] = partial_in[chunk, step * CAP + k]

        @pl.loop(0, UNITS_DEV // WIDE)
        def _(part):
            left = pl.multiple_of(part * WIDE, WIDE)
            wide = pl.ds(left, WIDE)
            hist[...] = jnp.dot(
                toeplitz[...], ext[pl.ds(start, 2 * LAG), wide], preferred_element_type=F32
            )
            for half in range(2):
                inner = slice(half * TILE, (half + 1) * TILE)
                cols = pl.ds(pl.multiple_of(left + half * TILE, TILE), TILE)
                tile = part * 2 + half

                coupling = jnp.zeros((LAG, TILE), F32)
                for step in range(PEERS):
                    first = names[step, unit * CAP]
                    second = names[step, unit * CAP + 1]
                    at = jnp.where(
                        first == tile,
                        step * CAP,
                        jnp.where(second == tile, step * CAP + 1, SLOTS),
                    )
                    coupling = coupling + stage[at].astype(F32)
                resid = ext[spike_rows, cols].astype(F32) - jnp.exp(base[rows, cols] + coupling)
                rounded = resid.astype(BF16)
                resid_tiles[tile] = rounded
                resid_rows[:, cols] = rounded
                stats[NB : NB + 1, cols] += jnp.sum(resid, axis=0, keepdims=True)
                for b in range(NB):
                    h = hist[b * LAG : (b + 1) * LAG, inner]
                    stats[b : b + 1, cols] += jnp.sum(h * resid, axis=0, keepdims=True)

        @pl.loop(1, PEERS + 1)
        def _(visit):
            step = offset(visit)
            first = jnp.minimum(names[step, unit * CAP], TILES_DEV - 1)
            second = jnp.maximum(names[step, unit * CAP + 1], 0)
            resid_out[chunk, step * CAP] = resid_tiles[first]
            resid_out[chunk, step * CAP + 1] = resid_tiles[second]

            @pl.when(step > 0)
            def _():
                resid_copy(chunk, step).start()

        for block in range(TM):
            stim_sum[block] += lax.dot_general(
                stim[rows, :],
                resid_rows[:, block * TILE : (block + 1) * TILE],
                (((0,), (0,)), ((), ())),
                preferred_element_type=F32,
            )

    def stats_copy(step):
        return pltpu.make_async_remote_copy(
            src_ref=stats,
            dst_ref=stats_in.at[tm],
            send_sem=sem_stats_send.at[step],
            recv_sem=sem_stats_recv.at[step],
            device_id=(unit, around(step)),
            device_id_type=MESH,
        )

    def stim_copy(step):
        return pltpu.make_async_remote_copy(
            src_ref=stim_sum.at[around(step)],
            dst_ref=stim_in.at[step],
            send_sem=sem_stim_send.at[step],
            recv_sem=sem_stim_recv.at[step],
            device_id=(unit, around(step)),
            device_id_type=MESH,
        )

    @pl.loop(1, TM)
    def _(step):
        stats_copy(step).start()
        stim_copy(step).start()

    grad[...] = jnp.zeros_like(grad)

    @pl.loop(0, CHUNKS)
    def _(turn):
        chunk = lax.rem(turn + 1, CHUNKS)
        rows = pl.ds(pl.multiple_of(chunk * LAG, LAG), LAG)

        for k in range(CAP):
            stage[k] = resid_out[chunk, k]

        @pl.loop(1, PEERS)
        def _(step):
            resid_copy(chunk, step).wait_recv()
            for k in range(CAP):
                stage[step * CAP + k] = resid_in[chunk, step * CAP + k]

        for s in range(TILES_DEV):
            chosen = jnp.concatenate([stage[slot_at[s * FAN + f]] for f in range(FAN)], axis=1)
            grad[s] += lax.dot_general(
                mixed[rows, s * TILE : (s + 1) * TILE],
                chosen,
                (((0,), (0,)), ((), ())),
                preferred_element_type=F32,
            )

    share = TILE // TM

    def pair_copy(z):
        return pltpu.make_async_remote_copy(
            src_ref=grad.at[:, pl.ds(pl.multiple_of((z * 2 + 1 - core) * share, share), share)],
            dst_ref=pair_in.at[z],
            send_sem=sem_pair.at[0, z],
            recv_sem=sem_pair.at[1, z],
            device_id=(unit, here_z * 2 + 1 - core),
            device_id_type=MESH,
        )

    def zed_copy(step):
        z = lax.rem(here_z + step, SIDE)
        return pltpu.make_async_remote_copy(
            src_ref=pair_out.at[z],
            dst_ref=zed_in.at[step],
            send_sem=sem_zed.at[0, step],
            recv_sem=sem_zed.at[1, step],
            device_id=(unit, z * 2 + core),
            device_id_type=MESH,
        )

    for step in (1, 2, 3, 0):
        pair_copy(lax.rem(here_z + step, SIDE)).start()

    def both(z):
        kept = pl.ds(pl.multiple_of((z * 2 + core) * share, share), share)
        return grad[:, kept, :] + pair_in[z]

    for step in (1, 2, 3):
        z = lax.rem(here_z + step, SIDE)
        pair_copy(z).wait_recv()
        pair_out[z] = both(z).astype(pair_out.dtype)
        zed_copy(step).start()
    pair_copy(here_z).wait_recv()
    final = both(here_z)

    time_total = float(TIME_DEV * TM)
    stats_in[tm] = stats[...]

    @pl.loop(1, TM)
    def _(step):
        stats_copy(step).wait()
        stim_copy(step).wait()

    total = stats_in[0]
    for block in range(1, TM):
        total = total + stats_in[block]
    out_hist[...] = total[:NB] / time_total
    out_bias[...] = total[NB : NB + 1] / time_total
    stim_total = stim_sum[tm]
    for step in range(1, TM):
        stim_total = stim_total + stim_in[step]
    out_stim[...] = stim_total / time_total

    for step in (1, 2, 3):
        zed_copy(step).wait_recv()
        final = final + zed_in[step].astype(F32)
    final = final / time_total
    for f in range(FAN):
        out_coupling[:, f] = final[:, :, f * TILE : (f + 1) * TILE]

    @pl.loop(0, CHUNKS)
    def _(chunk):
        @pl.loop(1, PEERS)
        def _(step):
            partial_copy(chunk, step).wait_send()
            resid_copy(chunk, step).wait_send()

    @pl.loop(0, SIDE)
    def _(z):
        pair_copy(z).wait_send()

    for step in (1, 2, 3):
        zed_copy(step).wait_send()


def shards(
    spikes, stimulus, bias, hist_weight, stim_filter, coupling_mix, coupling_target, coupling_weight
):
    smem = pl.BlockSpec(memory_space=pltpu.SMEM)
    vmem = pl.BlockSpec(memory_space=pltpu.VMEM)
    anywhere = pl.BlockSpec(memory_space=pl.ANY)
    named, weight_at, slot_at = pl.pallas_call(
        plan_kernel,
        out_shape=[
            jax.ShapeDtypeStruct((SLOTS,), jnp.int32),
            jax.ShapeDtypeStruct((SLOTS * TILES_DEV,), jnp.int32),
            jax.ShapeDtypeStruct((ENTRIES,), jnp.int32),
        ],
        in_specs=[smem],
        out_specs=[smem] * 3,
    )(coupling_target)
    dma = pltpu.SemaphoreType.DMA
    grad_bias, grad_hist, grad_stim, grad_coupling = pl.pallas_call(
        main_kernel,
        out_shape=[
            jax.ShapeDtypeStruct((1, UNITS_DEV), F32),
            jax.ShapeDtypeStruct((NB, UNITS_DEV), F32),
            jax.ShapeDtypeStruct((STIM, TILE), F32),
            jax.ShapeDtypeStruct((TILES_DEV, FAN, TILE // TM, TILE), F32),
        ],
        in_specs=[smem] * 4 + [vmem] * 5 + [anywhere, vmem],
        out_specs=[vmem] * 4,
        scratch_shapes=[
            pltpu.VMEM((TIME_DEV + LAG, UNITS_DEV), BF16),
            pltpu.VMEM((LAG, UNITS_DEV), BF16),
            pltpu.VMEM((ENTRIES + 1, TILE, TILE), BF16),
            pltpu.VMEM((NB * LAG, WIDE), F32),
            pltpu.VMEM((TIME_DEV, UNITS_DEV), BF16),
            pltpu.VMEM((TIME_DEV, UNITS_DEV), F32),
            pltpu.VMEM((CHUNKS, SLOTS, LAG, TILE), BF16),
            pltpu.VMEM((CHUNKS, SLOTS, LAG, TILE), BF16),
            pltpu.VMEM((SLOTS + 1, LAG, TILE), BF16),
            pltpu.VMEM((TILES_DEV, LAG, TILE), BF16),
            pltpu.VMEM((LAG, UNITS_DEV), BF16),
            pltpu.VMEM((CHUNKS, SLOTS, LAG, TILE), BF16),
            pltpu.VMEM((CHUNKS, SLOTS, LAG, TILE), BF16),
            pltpu.SMEM((PEERS, SLOTS), jnp.int32),
            pltpu.VMEM((TILES_DEV, TILE, FAN * TILE), F32),
            pltpu.VMEM((16, UNITS_DEV), F32),
            pltpu.VMEM((TM, 16, UNITS_DEV), F32),
            pltpu.VMEM((TM, STIM, TILE), F32),
            pltpu.VMEM((TM, STIM, TILE), F32),
            pltpu.VMEM((SIDE, TILES_DEV, TILE // TM, FAN * TILE), F32),
            pltpu.VMEM((SIDE, TILES_DEV, TILE // TM, FAN * TILE), F32),
            pltpu.VMEM((SIDE, TILES_DEV, TILE // TM, FAN * TILE), F32),
            dma((1,)),
            dma((2,)),
            dma((2, PEERS)),
            dma((CHUNKS, PEERS)),
            dma((CHUNKS, PEERS)),
            dma((CHUNKS, PEERS)),
            dma((CHUNKS, PEERS)),
            dma((TM,)),
            dma((TM,)),
            dma((TM,)),
            dma((TM,)),
            dma((2, SIDE)),
            dma((2, SIDE)),
        ],
        compiler_params=pltpu.CompilerParams(
            collective_id=0, has_side_effects=True, vmem_limit_bytes=56 * 1024 * 1024
        ),
    )(
        named,
        weight_at,
        slot_at,
        coupling_mix,
        spikes,
        stimulus,
        bias.reshape(1, UNITS_DEV),
        hist_weight,
        stim_filter,
        coupling_weight.reshape(ENTRIES, TILE, TILE),
        jnp.asarray(toeplitz_table()),
    )
    return (grad_bias.reshape(UNITS_DEV), grad_hist, grad_stim.T, grad_coupling)


def solution(mesh):
    return jax.shard_map(
        shards,
        mesh=mesh,
        in_specs=(
            P("tm", "unit"),
            P("tm", None),
            P("unit"),
            P(None, "unit"),
            P("unit", None),
            P(),
            P("unit", None),
            P("unit", None, None, None),
        ),
        out_specs=(
            P("unit"),
            P(None, "unit"),
            P(("unit", "tm"), None),
            P("unit", None, "tm", None),
        ),
        check_vma=False,
    )
```

time: 289 us -> 143 us (0.49); the launches traced: 284 us -> 142 us
  Pallas kernels: 0 us -> 131 us
  waiting for transfers between devices: 113 us -> 0 us
  matrix products: 43.8 us -> 0 us
  starting transfers between devices: 35.4 us -> 0 us
  local copies, waits for them, and re-layouts: 39.7 us -> 10.5 us
  blocking collectives: 21.7 us -> 0 us
  other arithmetic: 16 us -> 0 us
  between operations: 14.3 us -> 0.65 us
    pallas_call x0 -> x2, Pallas kernels: none -> 131 us  [the longest x1 126 us: shards(): pl.pallas_call(main_kernel, out_shape=[jax.ShapeDtypeStruct((1, UNITS_DEV...]
    all_to_all x3 -> x0, waiting for transfers between devices: 107 us -> none  [the longest x1 55.1 us: shards(): lax.all_to_all(outgoing.reshape(unit_count, CAP, time_dev, TILE), 'unit',...]
    dot_general x9 -> x0, matrix products: 43.8 us -> none  [the longest x1 13.8 us: shards(): jnp.einsum('tsk,cskn->ctn', mixed_tiles, slot_weight, preferred_element_t...]
    all_to_all x3 -> x0, starting transfers between devices: 30.8 us -> none  [the longest x1 16.2 us: shards(): lax.all_to_all(outgoing.reshape(unit_count, CAP, time_dev, TILE), 'unit',...]
    psum x1 -> x0, blocking collectives: 21.7 us -> none  [shards(): lax.psum((jnp.sum(resid, axis=0), jnp.sum(history_blocks * resid[None, :,...]
    all_to_all x4 -> x0, local copies, waits for them, and re-layouts: 19.5 us -> none  [the longest x1 11.3 us: shards(): lax.all_to_all(partials.reshape(unit_count, CAP, time_dev, TILE), 'unit',...]
    reduce_sum x3 -> x0, other arithmetic: 8.95 us -> none  [the longest x1 8.63 us: shards(): jnp.sum(history_blocks * resid[None, :, :], axis=1)]
    reshape x2 -> x0, local copies, waits for them, and re-layouts: 8.11 us -> none  [the longest x1 8.03 us: shards(): outgoing.reshape(unit_count, CAP, time_dev, TILE)]
  transfers between devices with their start and end apart: 6 -> 0, of which waited for: 3 -> 0; matrix products, arithmetic and copies ran while one was open for 24% -> 0% of each run, Pallas kernels for 0% -> 0%
where the time goes in v2:
time: 143 us; the launch traced here: 142 us
  Pallas kernels  131 us (92%)
  local copies, waits for them, and re-layouts  10.5 us (7%)
    pallas_call x1, Pallas kernels, shards(): pl.pallas_call(main_kernel, out_shape=[jax.ShapeDtypeStruct((1, UNITS_DEV...  126 us
    unnamed x7, local copies, waits for them, and re-layouts  10.5 us
    pallas_call x1, Pallas kernels, shards(): pl.pallas_call(plan_kernel, out_shape=[jax.ShapeDtypeStruct((SLOTS,), jnp...  5.15 us

profile of v2, /device:TPU:1, one launch (start us, length us, event | category | flops | bytes accessed | tf_op | source)
XLA Modules:
  0.0 142.2 jit_solution(14510243606421827553)
XLA Ops:
  0.6 1.3 copy.13.target
  2.0 5.2 %shard_map.120 = (s32[32]{0:T(128)}, s32[256]{0:T(256)}, s32[32]{0:T(128)}) custom-call(s32[8,4]{1,0:T(8,128)} %copy.13.target), custom_call_target="tpu_custom_call" | custom-call | tf_op jit(solution)/shard_map/pallas_call | solution.py:500
  7.1 1.6 %copy.14.stim = bf16[512,64]{1,0:T(8,128)(2,1)} copy(bf16[512,64]{0,1:T(8,128)(2,1)} %param.10) | data formatting | bytes 131072 | tf_op args[1]
  8.7 1.7 %copy.15.filt = bf16[1024,64]{1,0:T(8,128)(2,1)} copy(bf16[1024,64]{0,1:T(8,128)(2,1)} %param.13) | data formatting | bytes 262144 | tf_op args[4]
  10.5 125.9 %shard_map.121 = (f32[1,1024]{1,0:T(1,128)}, f32[10,1024]{1,0:T(8,128)}, f32[64,128]{1,0:T(8,128)}, f32[8,4,16,128]{3,2,1,0:T(8,128)}) custom-call(s32[32]{0:T(128)} %get-tuple-element.11.named, s32[256]{0:T(256)} %get-tuple-element.12.weight_at, s32[32]{0:T(128)} %get-tuple-element.13.slot_at, f32[10]{0:T(128)} %mix.1, s32[512,1024]{1,0:T(8,128)} %spikes.1, ...), custom_call_target="tpu_custom_call" | custom-call | tf_op jit(solution)/shard_map/pallas_call | solution.py:511
  136.4 1.3 copy.20
  137.7 1.5 %copy.21 = f32[10,1024]{1,0:T(8,128)} copy(f32[10,1024]{1,0:T(8,128)} %get-tuple-element.23) | data formatting | bytes 81920
  139.2 1.4 copy.22
  140.6 1.7 %copy.23 = f32[8,4,16,128]{3,2,1,0:T(8,128)} copy(f32[8,4,16,128]{3,2,1,0:T(8,128)} %get-tuple-element.25) | data formatting | bytes 524288

commit v3 on v2

--- a/solution.py
+++ b/solution.py
@@ -45,62 +45,31 @@
     return table.reshape(NB * LAG, 2 * LAG).astype(ml_dtypes.bfloat16)
 
 
-def plan_kernel(target, named, weight_at, slot_at):
-    unit = lax.axis_index("unit")
-    here_x, here_y = unit // SIDE, unit % SIDE
-
-    @pl.loop(0, PEERS)
-    def _(owner):
-        named[owner * CAP] = TILES_DEV
-        named[owner * CAP + 1] = -1
-
-    @pl.loop(0, SLOTS * TILES_DEV)
-    def _(place):
-        weight_at[place] = ENTRIES
-
-    @pl.loop(0, ENTRIES)
-    def _(entry):
-        tile = target[entry // FAN, entry % FAN]
-        at = (tile // TILES_DEV) * CAP
-        local = tile % TILES_DEV
-        named[at] = jnp.minimum(named[at], local)
-        named[at + 1] = jnp.maximum(named[at + 1], local)
-
-    @pl.loop(0, ENTRIES)
-    def _(entry):
-        tile = target[entry // FAN, entry % FAN]
-        owner = tile // TILES_DEV
-        local = tile % TILES_DEV
-        rank = (local == named[owner * CAP + 1]).astype(jnp.int32)
-        step_x = lax.rem(owner // SIDE - here_x + SIDE, SIDE)
-        step_y = lax.rem(owner % SIDE - here_y + SIDE, SIDE)
-        slot = (step_x * SIDE + step_y) * CAP + rank
-        slot_at[entry] = slot
-        weight_at[slot * TILES_DEV + entry // FAN] = entry
-
-
 def main_kernel(
-    named,
-    weight_at,
-    slot_at,
+    target,
     mix,
+    spikes_hbm,
+    stim_hbm,
+    bias_hbm,
+    hist_weight_hbm,
+    filt_hbm,
+    weights_hbm,
+    toeplitz_hbm,
+    out_stats,
+    out_stim,
+    out_coupling,
     spikes,
     stim,
     bias,
     hist_weight,
     filt,
-    weights_hbm,
     toeplitz,
-    out_bias,
-    out_hist,
-    out_stim,
-    out_coupling,
+    blend_filter,
     ext,
     halo,
     weights,
     hist,
     mixed,
-    base,
     partial_out,
     partial_in,
     stage,
@@ -108,6 +77,7 @@
     resid_rows,
     resid_out,
     resid_in,
+    named,
     names,
     grad,
     stats,
@@ -117,7 +87,8 @@
     pair_in,
     pair_out,
     zed_in,
-    sem_weights,
+    sem_load,
+    sem_spikes,
     sem_halo,
     sem_names,
     sem_a_send,
@@ -164,20 +135,68 @@
     def _(step):
         pl.semaphore_signal(barrier, inc=1, device_id=(unit, around(step)), device_id_type=MESH)
 
-    weights_copy = pltpu.make_async_copy(
-        weights_hbm, weights.at[pl.ds(0, ENTRIES)], sem_weights.at[0]
-    )
-    weights_copy.start()
+    def spikes_copy(chunk):
+        rows = pl.ds(pl.multiple_of(chunk * LAG, LAG), LAG)
+        return pltpu.make_async_copy(
+            spikes_hbm.at[rows, :], spikes.at[rows, :], sem_spikes.at[chunk]
+        )
+
+    loads = [
+        pltpu.make_async_copy(source, place, sem_load.at[k])
+        for k, (source, place) in enumerate(
+            (
+                (toeplitz_hbm, toeplitz),
+                (weights_hbm, weights.at[pl.ds(0, ENTRIES)]),
+                (stim_hbm, stim),
+                (bias_hbm, bias),
+                (hist_weight_hbm, hist_weight),
+                (filt_hbm, filt),
+            )
+        )
+    ]
+    spikes_copy(0).start()
+    spikes_copy(1).start()
+    loads[0].start()
+    spikes_copy(3).start()
+    loads[1].start()
+    spikes_copy(2).start()
+    for load in loads[2:]:
+        load.start()
+
+    @pl.loop(0, PEERS)
+    def _(owner):
+        first, last = owner * TILES_DEV, owner * TILES_DEV + TILES_DEV - 1
+        low, high = jnp.int32(PEERS * TILES_DEV), jnp.int32(-1)
+        for s in range(TILES_DEV):
+            for f in range(FAN):
+                tile = target[f, s]
+                low = jnp.where(tile >= first, jnp.minimum(low, tile), low)
+                high = jnp.where(tile <= last, jnp.maximum(high, tile), high)
+        named[owner * CAP] = low
+        named[owner * CAP + 1] = high
+
     weights[ENTRIES] = jnp.zeros((TILE, TILE), BF16)
     stage[SLOTS] = jnp.zeros((TILE, TILE), BF16)
     stats[...] = jnp.zeros_like(stats)
     stim_sum[...] = jnp.zeros_like(stim_sum)
-
-    @pl.loop(0, CHUNKS)
-    def _(chunk):
-        rows = pl.ds(pl.multiple_of(chunk * LAG, LAG), LAG)
-        later = pl.ds(pl.multiple_of(chunk * LAG + LAG, LAG), LAG)
-        ext[later, :] = spikes[rows, :].astype(BF16)
+    grad[...] = jnp.zeros_like(grad)
+
+    def take_spikes(chunk):
+        spikes_copy(chunk).wait()
+        ext[(chunk + 1) * LAG : (chunk + 2) * LAG, :] = spikes[
+            chunk * LAG : (chunk + 1) * LAG, :
+        ].astype(BF16)
+
+    take_spikes(0)
+    take_spikes(1)
+    loads[0].wait()
+    combined = jnp.zeros((LAG, 2 * LAG), F32)
+    for b in range(NB):
+        combined = combined + mix[b] * toeplitz[b * LAG : (b + 1) * LAG, :].astype(F32)
+    upper = combined.astype(BF16)
+    blend_filter[:LAG, :] = upper
+    blend_filter[LAG:, :] = (combined - upper.astype(F32)).astype(BF16)
+    take_spikes(3)
 
     pl.semaphore_wait(barrier, PEERS - 1 + TM - 1)
 
@@ -227,7 +246,7 @@
             device_id_type=MESH,
         )
 
-    weights_copy.wait()
+    loads[1].wait()
 
     @pl.loop(0, CHUNKS)
     def _(turn):
@@ -235,10 +254,78 @@
         start = pl.multiple_of(chunk * LAG, LAG)
         rows = pl.ds(start, LAG)
 
+        @pl.when(turn == 1)
+        def _():
+            take_spikes(2)
+
         @pl.when(turn == CHUNKS - 1)
         def _():
             halo_copy.wait()
             ext[pl.ds(0, LAG), :] = halo[...] * jnp.minimum(tm, 1).astype(BF16)
+
+        @pl.loop(0, UNITS_DEV // WIDE)
+        def _(part):
+            wide = pl.ds(pl.multiple_of(part * WIDE, WIDE), WIDE)
+            both = jnp.dot(
+                blend_filter[...], ext[pl.ds(start, 2 * LAG), wide], preferred_element_type=F32
+            )
+            mixed[rows, wide] = (both[:LAG] + both[LAG:]).astype(BF16)
+
+        @pl.loop(1, PEERS + 1)
+        def _(visit):
+            step = offset(visit)
+            owner = ahead(step)
+            low, high = named[owner * CAP], named[owner * CAP + 1]
+
+            def weight_of(s, tile):
+                at = jnp.int32(ENTRIES)
+                for f in range(FAN):
+                    at = jnp.where(target[f, s] == tile, s * FAN + f, at)
+                return weights[at]
+
+            total = jnp.zeros((LAG, WIDE), F32)
+            for s in range(0, TILES_DEV, 2):
+                block = jnp.concatenate(
+                    [
+                        jnp.concatenate([weight_of(s, low), weight_of(s, high)], axis=1),
+                        jnp.concatenate([weight_of(s + 1, low), weight_of(s + 1, high)], axis=1),
+                    ],
+                    axis=0,
+                )
+                total = total + jnp.dot(
+                    mixed[rows, s * TILE : (s + 2) * TILE], block, preferred_element_type=F32
+                )
+            partial_out[chunk, step * CAP] = total[:, :TILE].astype(BF16)
+            partial_out[chunk, step * CAP + 1] = total[:, TILE:].astype(BF16)
+
+            @pl.when(step > 0)
+            def _():
+                partial_copy(chunk, step).start()
+
+    @pl.loop(1, PEERS)
+    def _(step):
+        names_copy(step).wait()
+
+    for k in range(CAP * PEERS):
+        names[0, k] = named[k]
+    for load in loads[2:]:
+        load.wait()
+
+    @pl.loop(0, CHUNKS)
+    def _(turn):
+        chunk = lax.rem(turn + 1, CHUNKS)
+        start = pl.multiple_of(chunk * LAG, LAG)
+        rows = pl.ds(start, LAG)
+        spike_rows = pl.ds(pl.multiple_of(start + LAG, LAG), LAG)
+
+        for k in range(CAP):
+            stage[k] = partial_out[chunk, k]
+
+        @pl.loop(1, PEERS)
+        def _(step):
+            partial_copy(chunk, step).wait_recv()
+            for k in range(CAP):
+                stage[step * CAP + k] = partial_in[chunk, step * CAP + k]
 
         @pl.loop(0, UNITS_DEV // WIDE)
         def _(part):
@@ -248,82 +335,17 @@
                 toeplitz[...], ext[pl.ds(start, 2 * LAG), wide], preferred_element_type=F32
             )
             drive = bias[:, wide] + lax.dot_general(
-                stim[rows, :],
-                filt[wide, :],
-                (((1,), (1,)), ((), ())),
-                preferred_element_type=F32,
+                stim[:, rows], filt[:, wide], (((0,), (0,)), ((), ())), preferred_element_type=F32
             )
             for half in range(2):
                 inner = slice(half * TILE, (half + 1) * TILE)
                 cols = pl.ds(pl.multiple_of(left + half * TILE, TILE), TILE)
-                blend = jnp.zeros((LAG, TILE), F32)
-                own = drive[:, inner]
+                tile = unit * TILES_DEV + part * 2 + half
+
+                logit = drive[:, inner]
                 for b in range(NB):
                     h = hist[b * LAG : (b + 1) * LAG, inner]
-                    blend = blend + mix[b] * h
-                    own = own + hist_weight[b : b + 1, cols] * h
-                mixed[rows, cols] = blend.astype(BF16)
-                base[rows, cols] = own
-
-        @pl.loop(1, PEERS + 1)
-        def _(visit):
-            step = offset(visit)
-            total = jnp.zeros((LAG, WIDE), F32)
-            for s in range(0, TILES_DEV, 2):
-                at = step * (CAP * TILES_DEV) + s
-                top = jnp.concatenate(
-                    [weights[weight_at[at]], weights[weight_at[at + TILES_DEV]]], axis=1
-                )
-                low = jnp.concatenate(
-                    [weights[weight_at[at + 1]], weights[weight_at[at + TILES_DEV + 1]]], axis=1
-                )
-                total = total + jnp.dot(
-                    mixed[rows, s * TILE : (s + 2) * TILE],
-                    jnp.concatenate([top, low], axis=0),
-                    preferred_element_type=F32,
-                )
-            partial_out[chunk, step * CAP] = total[:, :TILE].astype(BF16)
-            partial_out[chunk, step * CAP + 1] = total[:, TILE:].astype(BF16)
-
-            @pl.when(step > 0)
-            def _():
-                partial_copy(chunk, step).start()
-
-    @pl.loop(1, PEERS)
-    def _(step):
-        names_copy(step).wait()
-
-    for k in range(CAP * PEERS):
-        names[0, k] = named[k]
-
-    @pl.loop(0, CHUNKS)
-    def _(turn):
-        chunk = lax.rem(turn + 1, CHUNKS)
-        start = pl.multiple_of(chunk * LAG, LAG)
-        rows = pl.ds(start, LAG)
-        spike_rows = pl.ds(pl.multiple_of(start + LAG, LAG), LAG)
-
-        for k in range(CAP):
-            stage[k] = partial_out[chunk, k]
-
-        @pl.loop(1, PEERS)
-        def _(step):
-            partial_copy(chunk, step).wait_recv()
-            for k in range(CAP):
-                stage[step * CAP + k] = partial_in[chunk, step * CAP + k]
-
-        @pl.loop(0, UNITS_DEV // WIDE)
-        def _(part):
-            left = pl.multiple_of(part * WIDE, WIDE)
-            wide = pl.ds(left, WIDE)
-            hist[...] = jnp.dot(
-                toeplitz[...], ext[pl.ds(start, 2 * LAG), wide], preferred_element_type=F32
-            )
-            for half in range(2):
-                inner = slice(half * TILE, (half + 1) * TILE)
-                cols = pl.ds(pl.multiple_of(left + half * TILE, TILE), TILE)
-                tile = part * 2 + half
-
+                    logit = logit + hist_weight[b : b + 1, cols] * h
                 coupling = jnp.zeros((LAG, TILE), F32)
                 for step in range(PEERS):
                     first = names[step, unit * CAP]
@@ -334,9 +356,9 @@
                         jnp.where(second == tile, step * CAP + 1, SLOTS),
                     )
                     coupling = coupling + stage[at].astype(F32)
-                resid = ext[spike_rows, cols].astype(F32) - jnp.exp(base[rows, cols] + coupling)
+                resid = ext[spike_rows, cols].astype(F32) - jnp.exp(logit + coupling)
                 rounded = resid.astype(BF16)
-                resid_tiles[tile] = rounded
+                resid_tiles[part * 2 + half] = rounded
                 resid_rows[:, cols] = rounded
                 stats[NB : NB + 1, cols] += jnp.sum(resid, axis=0, keepdims=True)
                 for b in range(NB):
@@ -346,10 +368,10 @@
         @pl.loop(1, PEERS + 1)
         def _(visit):
             step = offset(visit)
-            first = jnp.minimum(names[step, unit * CAP], TILES_DEV - 1)
-            second = jnp.maximum(names[step, unit * CAP + 1], 0)
-            resid_out[chunk, step * CAP] = resid_tiles[first]
-            resid_out[chunk, step * CAP + 1] = resid_tiles[second]
+            for k in range(CAP):
+                tile = names[step, unit * CAP + k] - unit * TILES_DEV
+                tile = jnp.minimum(jnp.maximum(tile, 0), TILES_DEV - 1)
+                resid_out[chunk, step * CAP + k] = resid_tiles[tile]
 
             @pl.when(step > 0)
             def _():
@@ -357,9 +379,9 @@
 
         for block in range(TM):
             stim_sum[block] += lax.dot_general(
-                stim[rows, :],
+                stim[:, rows],
                 resid_rows[:, block * TILE : (block + 1) * TILE],
-                (((0,), (0,)), ((), ())),
+                (((1,), (0,)), ((), ())),
                 preferred_element_type=F32,
             )
 
@@ -388,7 +410,12 @@
         stats_copy(step).start()
         stim_copy(step).start()
 
-    grad[...] = jnp.zeros_like(grad)
+    def slot_of(s, f):
+        owner = target[f, s] // TILES_DEV
+        step_x = lax.rem(owner // SIDE - here_x + SIDE, SIDE)
+        step_y = lax.rem(owner % SIDE - here_y + SIDE, SIDE)
+        rank = (target[f, s] == named[owner * CAP + 1]).astype(jnp.int32)
+        return (step_x * SIDE + step_y) * CAP + rank
 
     @pl.loop(0, CHUNKS)
     def _(turn):
@@ -401,11 +428,12 @@
         @pl.loop(1, PEERS)
         def _(step):
             resid_copy(chunk, step).wait_recv()
+            partial_copy(chunk, step).wait_send()
             for k in range(CAP):
                 stage[step * CAP + k] = resid_in[chunk, step * CAP + k]
 
         for s in range(TILES_DEV):
-            chosen = jnp.concatenate([stage[slot_at[s * FAN + f]] for f in range(FAN)], axis=1)
+            chosen = jnp.concatenate([stage[slot_of(s, f)] for f in range(FAN)], axis=1)
             grad[s] += lax.dot_general(
                 mixed[rows, s * TILE : (s + 1) * TILE],
                 chosen,
@@ -451,7 +479,6 @@
     pair_copy(here_z).wait_recv()
     final = both(here_z)
 
-    time_total = float(TIME_DEV * TM)
     stats_in[tm] = stats[...]
 
     @pl.loop(1, TM)
@@ -462,25 +489,16 @@
     total = stats_in[0]
     for block in range(1, TM):
         total = total + stats_in[block]
-    out_hist[...] = total[:NB] / time_total
-    out_bias[...] = total[NB : NB + 1] / time_total
+    out_stats[...] = total
     stim_total = stim_sum[tm]
     for step in range(1, TM):
         stim_total = stim_total + stim_in[step]
-    out_stim[...] = stim_total / time_total
-
-    for step in (1, 2, 3):
-        zed_copy(step).wait_recv()
-        final = final + zed_in[step].astype(F32)
-    final = final / time_total
-    for f in range(FAN):
-        out_coupling[:, f] = final[:, :, f * TILE : (f + 1) * TILE]
+    out_stim[...] = stim_total
 
     @pl.loop(0, CHUNKS)
     def _(chunk):
         @pl.loop(1, PEERS)
         def _(step):
-            partial_copy(chunk, step).wait_send()
             resid_copy(chunk, step).wait_send()
 
     @pl.loop(0, SIDE)
@@ -488,7 +506,18 @@
         pair_copy(z).wait_send()
 
     for step in (1, 2, 3):
-        zed_copy(step).wait_send()
+        zed_copy(step).wait()
+        final = final + zed_in[step].astype(F32)
+    out_coupling[...] = final
+
+
+def finish_kernel(stats, stim, coupling, out_bias, out_hist, out_stim, out_coupling):
+    time_total = float(TIME_DEV * TM)
+    out_hist[...] = stats[:NB, :] / time_total
+    out_bias[...] = stats[NB : NB + 1, :] / time_total
+    out_stim[...] = stim[...] / time_total
+    for f in range(FAN):
+        out_coupling[:, f] = coupling[:, :, f * TILE : (f + 1) * TILE] / time_total
 
 
 def shards(
@@ -497,34 +526,30 @@
     smem = pl.BlockSpec(memory_space=pltpu.SMEM)
     vmem = pl.BlockSpec(memory_space=pltpu.VMEM)
     anywhere = pl.BlockSpec(memory_space=pl.ANY)
-    named, weight_at, slot_at = pl.pallas_call(
-        plan_kernel,
-        out_shape=[
-            jax.ShapeDtypeStruct((SLOTS,), jnp.int32),
-            jax.ShapeDtypeStruct((SLOTS * TILES_DEV,), jnp.int32),
-            jax.ShapeDtypeStruct((ENTRIES,), jnp.int32),
-        ],
-        in_specs=[smem],
-        out_specs=[smem] * 3,
-    )(coupling_target)
     dma = pltpu.SemaphoreType.DMA
-    grad_bias, grad_hist, grad_stim, grad_coupling = pl.pallas_call(
+    share = TILE // TM
+    sums = pl.pallas_call(
         main_kernel,
         out_shape=[
-            jax.ShapeDtypeStruct((1, UNITS_DEV), F32),
-            jax.ShapeDtypeStruct((NB, UNITS_DEV), F32),
+            jax.ShapeDtypeStruct((16, UNITS_DEV), F32),
             jax.ShapeDtypeStruct((STIM, TILE), F32),
-            jax.ShapeDtypeStruct((TILES_DEV, FAN, TILE // TM, TILE), F32),
+            jax.ShapeDtypeStruct((TILES_DEV, share, FAN * TILE), F32),
         ],
-        in_specs=[smem] * 4 + [vmem] * 5 + [anywhere, vmem],
-        out_specs=[vmem] * 4,
+        in_specs=[smem] * 2 + [anywhere] * 7,
+        out_specs=[vmem] * 3,
         scratch_shapes=[
+            pltpu.VMEM((TIME_DEV, UNITS_DEV), jnp.int32),
+            pltpu.VMEM((STIM, TIME_DEV), BF16),
+            pltpu.VMEM((1, UNITS_DEV), F32),
+            pltpu.VMEM((NB, UNITS_DEV), F32),
+            pltpu.VMEM((STIM, UNITS_DEV), BF16),
+            pltpu.VMEM((NB * LAG, 2 * LAG), BF16),
+            pltpu.VMEM((2 * LAG, 2 * LAG), BF16),
             pltpu.VMEM((TIME_DEV + LAG, UNITS_DEV), BF16),
             pltpu.VMEM((LAG, UNITS_DEV), BF16),
             pltpu.VMEM((ENTRIES + 1, TILE, TILE), BF16),
             pltpu.VMEM((NB * LAG, WIDE), F32),
             pltpu.VMEM((TIME_DEV, UNITS_DEV), BF16),
-            pltpu.VMEM((TIME_DEV, UNITS_DEV), F32),
             pltpu.VMEM((CHUNKS, SLOTS, LAG, TILE), BF16),
             pltpu.VMEM((CHUNKS, SLOTS, LAG, TILE), BF16),
             pltpu.VMEM((SLOTS + 1, LAG, TILE), BF16),
@@ -532,16 +557,18 @@
             pltpu.VMEM((LAG, UNITS_DEV), BF16),
             pltpu.VMEM((CHUNKS, SLOTS, LAG, TILE), BF16),
             pltpu.VMEM((CHUNKS, SLOTS, LAG, TILE), BF16),
+            pltpu.SMEM((SLOTS,), jnp.int32),
             pltpu.SMEM((PEERS, SLOTS), jnp.int32),
             pltpu.VMEM((TILES_DEV, TILE, FAN * TILE), F32),
             pltpu.VMEM((16, UNITS_DEV), F32),
             pltpu.VMEM((TM, 16, UNITS_DEV), F32),
             pltpu.VMEM((TM, STIM, TILE), F32),
             pltpu.VMEM((TM, STIM, TILE), F32),
-            pltpu.VMEM((SIDE, TILES_DEV, TILE // TM, FAN * TILE), F32),
-            pltpu.VMEM((SIDE, TILES_DEV, TILE // TM, FAN * TILE), F32),
-            pltpu.VMEM((SIDE, TILES_DEV, TILE // TM, FAN * TILE), F32),
-            dma((1,)),
+            pltpu.VMEM((SIDE, TILES_DEV, share, FAN * TILE), F32),
+            pltpu.VMEM((SIDE, TILES_DEV, share, FAN * TILE), BF16),
+            pltpu.VMEM((SIDE, TILES_DEV, share, FAN * TILE), BF16),
+            dma((6,)),
+            dma((CHUNKS,)),
             dma((2,)),
             dma((2, PEERS)),
             dma((CHUNKS, PEERS)),
@@ -559,18 +586,27 @@
             collective_id=0, has_side_effects=True, vmem_limit_bytes=56 * 1024 * 1024
         ),
     )(
-        named,
-        weight_at,
-        slot_at,
+        coupling_target.T,
         coupling_mix,
         spikes,
-        stimulus,
+        stimulus.T,
         bias.reshape(1, UNITS_DEV),
         hist_weight,
-        stim_filter,
+        stim_filter.T,
         coupling_weight.reshape(ENTRIES, TILE, TILE),
         jnp.asarray(toeplitz_table()),
     )
+    grad_bias, grad_hist, grad_stim, grad_coupling = pl.pallas_call(
+        finish_kernel,
+        out_shape=[
+            jax.ShapeDtypeStruct((1, UNITS_DEV), F32),
+            jax.ShapeDtypeStruct((NB, UNITS_DEV), F32),
+            jax.ShapeDtypeStruct((STIM, TILE), F32),
+            jax.ShapeDtypeStruct((TILES_DEV, FAN, share, TILE), F32),
+        ],
+        in_specs=[vmem] * 3,
+        out_specs=[vmem] * 4,
+    )(*sums)
     return (grad_bias.reshape(UNITS_DEV), grad_hist, grad_stim.T, grad_coupling)
 
 

time: 143 us -> 121 us (0.85)
  Pallas kernels: 131 us -> 120 us
  local copies, waits for them, and re-layouts: 10.5 us -> 0 us
    pallas_call x2, Pallas kernels: 131 us -> 120 us  [the longest x1 119 us: shards(): pl.pallas_call(main_kernel, out_shape=[jax.ShapeDtypeStruct((16, UNITS_DE...]
    unnamed x7 -> x0, local copies, waits for them, and re-layouts: 10.5 us -> none
where the time goes in v3:
time: 121 us
  Pallas kernels  120 us (99%)
    pallas_call x1, Pallas kernels, shards(): pl.pallas_call(main_kernel, out_shape=[jax.ShapeDtypeStruct((16, UNITS_DE...  119 us

profile of v3, /device:TPU:1, one launch (start us, length us, event | category | flops | bytes accessed | tf_op | source)
XLA Modules:
  0.0 121.1 jit_solution(2158252409937536630)
XLA Ops:
  0.6 118.7 %shard_map.120 = (f32[16,1024]{1,0:T(8,128)}, f32[64,128]{1,0:T(8,128)}, f32[8,16,512]{2,1,0:T(8,128)}) custom-call(s32[4,8]{1,0:T(4,128)} %bitcast.11, f32[10]{0:T(128)} %mix.1, s32[512,1024]{1,0:T(8,128)} %spikes_hbm.1, bf16[64,512]{1,0:T(8,128)(2,1)} %bitcast.9, f32[1,1024]{1,0:T(1,128)} %bitcast.10, f32[10,1024]{1,0:T(8,128)} %hist_weight_hbm.1, ...), custom_call_target="tpu_custom_call" | custom-call | tf_op jit(solution)/shard_map/pallas_call | solution.py:531
  119.3 1.8 %shard_map.121 = (f32[1,1024]{1,0:T(1,128)}, f32[10,1024]{1,0:T(8,128)}, f32[64,128]{1,0:T(8,128)}, f32[8,4,16,128]{3,2,1,0:T(8,128)}) custom-call(f32[16,1024]{1,0:T(8,128)} %get-tuple-element.11.stats, f32[64,128]{1,0:T(8,128)} %get-tuple-element.12.stim, f32[8,16,512]{2,1,0:T(8,128)} %get-tuple-element.13.coupling), custom_call_target="tpu_custom_call" | custom-call | tf_op jit(solution)/shard_map/pallas_call | solution.py:599

commit v4 on v3

--- a/solution.py
+++ b/solution.py
@@ -87,6 +87,7 @@
     pair_in,
     pair_out,
     zed_in,
+    final,
     sem_load,
     sem_spikes,
     sem_halo,
@@ -95,10 +96,8 @@
     sem_a_recv,
     sem_b_send,
     sem_b_recv,
-    sem_stats_send,
-    sem_stats_recv,
-    sem_stim_send,
-    sem_stim_recv,
+    sem_stats,
+    sem_stim,
     sem_pair,
     sem_zed,
 ):
@@ -196,8 +195,19 @@
     upper = combined.astype(BF16)
     blend_filter[:LAG, :] = upper
     blend_filter[LAG:, :] = (combined - upper.astype(F32)).astype(BF16)
+
+    def mix_rows(chunk):
+        start = pl.multiple_of(chunk * LAG, LAG)
+        for part in range(UNITS_DEV // WIDE):
+            wide = slice(part * WIDE, (part + 1) * WIDE)
+            both = jnp.dot(
+                blend_filter[...], ext[pl.ds(start, 2 * LAG), wide], preferred_element_type=F32
+            )
+            mixed[pl.ds(start, LAG), wide] = (both[:LAG] + both[LAG:]).astype(BF16)
+
+    mix_rows(1)
     take_spikes(3)
-
+    loads[1].wait()
     pl.semaphore_wait(barrier, PEERS - 1 + TM - 1)
 
     halo_copy = pltpu.make_async_remote_copy(
@@ -208,7 +218,6 @@
         device_id=(unit, around(1)),
         device_id_type=MESH,
     )
-    halo_copy.start()
 
     def names_copy(step):
         return pltpu.make_async_remote_copy(
@@ -220,33 +229,27 @@
             device_id_type=MESH,
         )
 
-    @pl.loop(1, PEERS)
-    def _(step):
-        names_copy(step).start()
-
-    def partial_copy(chunk, step):
-        pair = pl.ds(step * CAP, CAP)
+    def partial_copy(chunk, step, count=1):
+        pair = pl.ds(step * CAP, count * CAP)
         return pltpu.make_async_remote_copy(
             src_ref=partial_out.at[chunk, pair],
             dst_ref=partial_in.at[chunk, pair],
-            send_sem=sem_a_send.at[chunk, step],
-            recv_sem=sem_a_recv.at[chunk, step],
+            send_sem=sem_a_send.at[chunk],
+            recv_sem=sem_a_recv.at[chunk],
             device_id=(ahead(step), tm),
             device_id_type=MESH,
         )
 
-    def resid_copy(chunk, step):
-        pair = pl.ds(step * CAP, CAP)
+    def resid_copy(chunk, step, count=1):
+        pair = pl.ds(step * CAP, count * CAP)
         return pltpu.make_async_remote_copy(
             src_ref=resid_out.at[chunk, pair],
             dst_ref=resid_in.at[chunk, pair],
-            send_sem=sem_b_send.at[chunk, step],
-            recv_sem=sem_b_recv.at[chunk, step],
+            send_sem=sem_b_send.at[chunk],
+            recv_sem=sem_b_recv.at[chunk],
             device_id=(behind(step), tm),
             device_id_type=MESH,
         )
-
-    loads[1].wait()
 
     @pl.loop(0, CHUNKS)
     def _(turn):
@@ -263,13 +266,9 @@
             halo_copy.wait()
             ext[pl.ds(0, LAG), :] = halo[...] * jnp.minimum(tm, 1).astype(BF16)
 
-        @pl.loop(0, UNITS_DEV // WIDE)
-        def _(part):
-            wide = pl.ds(pl.multiple_of(part * WIDE, WIDE), WIDE)
-            both = jnp.dot(
-                blend_filter[...], ext[pl.ds(start, 2 * LAG), wide], preferred_element_type=F32
-            )
-            mixed[rows, wide] = (both[:LAG] + both[LAG:]).astype(BF16)
+        @pl.when(turn > 0)
+        def _():
+            mix_rows(chunk)
 
         @pl.loop(1, PEERS + 1)
         def _(visit):
@@ -302,6 +301,14 @@
             def _():
                 partial_copy(chunk, step).start()
 
+                @pl.when(turn == 0)
+                def _():
+                    names_copy(step).start()
+
+        @pl.when(turn == 0)
+        def _():
+            halo_copy.start()
+
     @pl.loop(1, PEERS)
     def _(step):
         names_copy(step).wait()
@@ -321,11 +328,8 @@
         for k in range(CAP):
             stage[k] = partial_out[chunk, k]
 
-        @pl.loop(1, PEERS)
-        def _(step):
-            partial_copy(chunk, step).wait_recv()
-            for k in range(CAP):
-                stage[step * CAP + k] = partial_in[chunk, step * CAP + k]
+        partial_copy(chunk, 1, PEERS - 1).wait_recv()
+        stage[CAP:SLOTS] = partial_in[chunk, CAP:]
 
         @pl.loop(0, UNITS_DEV // WIDE)
         def _(part):
@@ -388,9 +392,9 @@
     def stats_copy(step):
         return pltpu.make_async_remote_copy(
             src_ref=stats,
-            dst_ref=stats_in.at[tm],
-            send_sem=sem_stats_send.at[step],
-            recv_sem=sem_stats_recv.at[step],
+            dst_ref=stats_in.at[step],
+            send_sem=sem_stats.at[0],
+            recv_sem=sem_stats.at[1],
             device_id=(unit, around(step)),
             device_id_type=MESH,
         )
@@ -399,11 +403,22 @@
         return pltpu.make_async_remote_copy(
             src_ref=stim_sum.at[around(step)],
             dst_ref=stim_in.at[step],
-            send_sem=sem_stim_send.at[step],
-            recv_sem=sem_stim_recv.at[step],
+            send_sem=sem_stim.at[0],
+            recv_sem=sem_stim.at[1],
             device_id=(unit, around(step)),
             device_id_type=MESH,
         )
+
+    def all_arrived(place, sems):
+        others = place.at[pl.ds(1, TM - 1)]
+        pltpu.make_async_remote_copy(
+            src_ref=others,
+            dst_ref=others,
+            send_sem=sems.at[0],
+            recv_sem=sems.at[1],
+            device_id=(unit, around(1)),
+            device_id_type=MESH,
+        ).wait()
 
     @pl.loop(1, TM)
     def _(step):
@@ -417,98 +432,98 @@
         rank = (target[f, s] == named[owner * CAP + 1]).astype(jnp.int32)
         return (step_x * SIDE + step_y) * CAP + rank
 
-    @pl.loop(0, CHUNKS)
-    def _(turn):
-        chunk = lax.rem(turn + 1, CHUNKS)
-        rows = pl.ds(pl.multiple_of(chunk * LAG, LAG), LAG)
-
+    def take_resid(chunk):
         for k in range(CAP):
             stage[k] = resid_out[chunk, k]
-
-        @pl.loop(1, PEERS)
-        def _(step):
-            resid_copy(chunk, step).wait_recv()
-            partial_copy(chunk, step).wait_send()
-            for k in range(CAP):
-                stage[step * CAP + k] = resid_in[chunk, step * CAP + k]
-
+        partial_copy(chunk, 1, PEERS - 1).wait_send()
+        resid_copy(chunk, 1, PEERS - 1).wait_recv()
+        stage[CAP:SLOTS] = resid_in[chunk, CAP:]
+
+    def add_grad(chunk, s):
+        chosen = jnp.concatenate([stage[slot_of(s, f)] for f in range(FAN)], axis=1)
+        grad[s] += lax.dot_general(
+            mixed[pl.ds(pl.multiple_of(chunk * LAG, LAG), LAG), s * TILE : (s + 1) * TILE],
+            chosen,
+            (((0,), (0,)), ((), ())),
+            preferred_element_type=F32,
+        )
+
+    @pl.loop(1, CHUNKS)
+    def _(chunk):
+        take_resid(chunk)
         for s in range(TILES_DEV):
-            chosen = jnp.concatenate([stage[slot_of(s, f)] for f in range(FAN)], axis=1)
-            grad[s] += lax.dot_general(
-                mixed[rows, s * TILE : (s + 1) * TILE],
-                chosen,
-                (((0,), (0,)), ((), ())),
-                preferred_element_type=F32,
-            )
+            add_grad(chunk, s)
 
     share = TILE // TM
-
-    def pair_copy(z):
+    half_tiles = TILES_DEV // 2
+
+    def pair_copy(half, z):
+        given = pl.ds(pl.multiple_of((z * 2 + 1 - core) * share, share), share)
         return pltpu.make_async_remote_copy(
-            src_ref=grad.at[:, pl.ds(pl.multiple_of((z * 2 + 1 - core) * share, share), share)],
-            dst_ref=pair_in.at[z],
-            send_sem=sem_pair.at[0, z],
-            recv_sem=sem_pair.at[1, z],
+            src_ref=grad.at[pl.ds(half * half_tiles, half_tiles), given],
+            dst_ref=pair_in.at[half, z],
+            send_sem=sem_pair.at[0, half, z],
+            recv_sem=sem_pair.at[1, half, z],
             device_id=(unit, here_z * 2 + 1 - core),
             device_id_type=MESH,
         )
 
-    def zed_copy(step):
+    def zed_copy(half, step):
         z = lax.rem(here_z + step, SIDE)
         return pltpu.make_async_remote_copy(
-            src_ref=pair_out.at[z],
-            dst_ref=zed_in.at[step],
-            send_sem=sem_zed.at[0, step],
-            recv_sem=sem_zed.at[1, step],
+            src_ref=pair_out.at[half, z],
+            dst_ref=zed_in.at[half, step],
+            send_sem=sem_zed.at[0, half, step],
+            recv_sem=sem_zed.at[1, half, step],
             device_id=(unit, z * 2 + core),
             device_id_type=MESH,
         )
 
-    for step in (1, 2, 3, 0):
-        pair_copy(lax.rem(here_z + step, SIDE)).start()
-
-    def both(z):
+    def both(half, z):
         kept = pl.ds(pl.multiple_of((z * 2 + core) * share, share), share)
-        return grad[:, kept, :] + pair_in[z]
-
-    for step in (1, 2, 3):
-        z = lax.rem(here_z + step, SIDE)
-        pair_copy(z).wait_recv()
-        pair_out[z] = both(z).astype(pair_out.dtype)
-        zed_copy(step).start()
-    pair_copy(here_z).wait_recv()
-    final = both(here_z)
-
-    stats_in[tm] = stats[...]
-
-    @pl.loop(1, TM)
-    def _(step):
-        stats_copy(step).wait()
-        stim_copy(step).wait()
-
-    total = stats_in[0]
+        return grad[half * half_tiles : (half + 1) * half_tiles, kept, :] + pair_in[half, z]
+
+    take_resid(0)
+    for half in range(2):
+        for s in range(half * half_tiles, (half + 1) * half_tiles):
+            add_grad(0, s)
+        for step in (2, 1, 3, 0):
+            pair_copy(half, lax.rem(here_z + step, SIDE)).start()
+    for half in range(2):
+        for step in (2, 1, 3):
+            z = lax.rem(here_z + step, SIDE)
+            pair_copy(half, z).wait_recv()
+            pair_out[half, z] = both(half, z).astype(pair_out.dtype)
+            zed_copy(half, step).start()
+    for half in range(2):
+        pair_copy(half, here_z).wait_recv()
+        final[half * half_tiles : (half + 1) * half_tiles] = both(half, here_z)
+
+    all_arrived(stats_in, sem_stats)
+    all_arrived(stim_in, sem_stim)
+    stats_in[0] = stats[...]
+    total = stats_in[tm]
     for block in range(1, TM):
-        total = total + stats_in[block]
+        total = total + stats_in[lax.rem(tm - block + TM, TM)]
     out_stats[...] = total
     stim_total = stim_sum[tm]
     for step in range(1, TM):
         stim_total = stim_total + stim_in[step]
     out_stim[...] = stim_total
 
-    @pl.loop(0, CHUNKS)
-    def _(chunk):
-        @pl.loop(1, PEERS)
-        def _(step):
-            resid_copy(chunk, step).wait_send()
-
-    @pl.loop(0, SIDE)
-    def _(z):
-        pair_copy(z).wait_send()
-
-    for step in (1, 2, 3):
-        zed_copy(step).wait()
-        final = final + zed_in[step].astype(F32)
-    out_coupling[...] = final
+    for chunk in range(CHUNKS):
+        resid_copy(chunk, 1, PEERS - 1).wait_send()
+
+    for half in range(2):
+        for z in range(SIDE):
+            pair_copy(half, z).wait_send()
+    for half in range(2):
+        tiles = slice(half * half_tiles, (half + 1) * half_tiles)
+        total = final[tiles]
+        for step in (1, 2, 3):
+            zed_copy(half, step).wait()
+            total = total + zed_in[half, step].astype(F32)
+        out_coupling[tiles] = total
 
 
 def finish_kernel(stats, stim, coupling, out_bias, out_hist, out_stim, out_coupling):
@@ -564,23 +579,22 @@
             pltpu.VMEM((TM, 16, UNITS_DEV), F32),
             pltpu.VMEM((TM, STIM, TILE), F32),
             pltpu.VMEM((TM, STIM, TILE), F32),
-            pltpu.VMEM((SIDE, TILES_DEV, share, FAN * TILE), F32),
-            pltpu.VMEM((SIDE, TILES_DEV, share, FAN * TILE), BF16),
-            pltpu.VMEM((SIDE, TILES_DEV, share, FAN * TILE), BF16),
+            pltpu.VMEM((2, SIDE, TILES_DEV // 2, share, FAN * TILE), F32),
+            pltpu.VMEM((2, SIDE, TILES_DEV // 2, share, FAN * TILE), BF16),
+            pltpu.VMEM((2, SIDE, TILES_DEV // 2, share, FAN * TILE), BF16),
+            pltpu.VMEM((TILES_DEV, share, FAN * TILE), F32),
             dma((6,)),
             dma((CHUNKS,)),
             dma((2,)),
             dma((2, PEERS)),
-            dma((CHUNKS, PEERS)),
-            dma((CHUNKS, PEERS)),
-            dma((CHUNKS, PEERS)),
-            dma((CHUNKS, PEERS)),
-            dma((TM,)),
-            dma((TM,)),
-            dma((TM,)),
-            dma((TM,)),
-            dma((2, SIDE)),
-            dma((2, SIDE)),
+            dma((CHUNKS,)),
+            dma((CHUNKS,)),
+            dma((CHUNKS,)),
+            dma((CHUNKS,)),
+            dma((2,)),
+            dma((2,)),
+            dma((2, 2, SIDE)),
+            dma((2, 2, SIDE)),
         ],
         compiler_params=pltpu.CompilerParams(
             collective_id=0, has_side_effects=True, vmem_limit_bytes=56 * 1024 * 1024

time: 121 us -> 118 us (0.975)
  Pallas kernels: 120 us -> 117 us
    pallas_call x1, Pallas kernels: 119 us -> 115 us  [shards(): pl.pallas_call(main_kernel, out_shape=[jax.ShapeDtypeStruct((16, UNITS_DE...]
where the time goes in v4:
time: 118 us
  Pallas kernels  117 us (99%)
    pallas_call x1, Pallas kernels, shards(): pl.pallas_call(main_kernel, out_shape=[jax.ShapeDtypeStruct((16, UNITS_DE...  115 us

profile of v4, /device:TPU:1, one launch (start us, length us, event | category | flops | bytes accessed | tf_op | source)
XLA Modules:
  0.0 117.7 jit_solution(2196756617703586458)
XLA Ops:
  0.6 115.2 %shard_map.120 = (f32[16,1024]{1,0:T(8,128)}, f32[64,128]{1,0:T(8,128)}, f32[8,16,512]{2,1,0:T(8,128)}) custom-call(s32[4,8]{1,0:T(4,128)} %bitcast.11, f32[10]{0:T(128)} %mix.1, s32[512,1024]{1,0:T(8,128)} %spikes_hbm.1, bf16[64,512]{1,0:T(8,128)(2,1)} %bitcast.9, f32[1,1024]{1,0:T(1,128)} %bitcast.10, f32[10,1024]{1,0:T(8,128)} %hist_weight_hbm.1, ...), custom_call_target="tpu_custom_call" | custom-call | tf_op jit(solution)/shard_map/pallas_call | solution.py:546
  115.9 1.8 %shard_map.121 = (f32[1,1024]{1,0:T(1,128)}, f32[10,1024]{1,0:T(8,128)}, f32[64,128]{1,0:T(8,128)}, f32[8,4,16,128]{3,2,1,0:T(8,128)}) custom-call(f32[16,1024]{1,0:T(8,128)} %get-tuple-element.11.stats, f32[64,128]{1,0:T(8,128)} %get-tuple-element.12.stim, f32[8,16,512]{2,1,0:T(8,128)} %get-tuple-element.13.coupling), custom_call_target="tpu_custom_call" | custom-call | tf_op jit(solution)/shard_map/pallas_call | solution.py:613

commit v5 on v4

--- a/solution.py
+++ b/solution.py
@@ -17,6 +17,7 @@
 LAG = 128
 SIDE = 4
 PEERS = SIDE * SIDE
+HALF = LAG // 2
 SLOTS = PEERS * CAP
 TILES_DEV = 8
 UNITS_DEV = TILES_DEV * TILE
@@ -72,12 +73,15 @@
     mixed,
     partial_out,
     partial_in,
+    dense,
+    far_in,
+    near_in,
     stage,
-    resid_tiles,
     resid_rows,
     resid_out,
+    got,
+    pick,
     resid_in,
-    named,
     names,
     grad,
     stats,
@@ -92,10 +96,8 @@
     sem_spikes,
     sem_halo,
     sem_names,
-    sem_a_send,
-    sem_a_recv,
-    sem_b_send,
-    sem_b_recv,
+    sem_send,
+    sem_recv,
     sem_stats,
     sem_stim,
     sem_pair,
@@ -106,20 +108,17 @@
     here_x, here_y = unit // SIDE, unit % SIDE
     here_z, core = tm // 2, tm % 2
 
+    def device(step_x, step_y):
+        return lax.rem(here_x + step_x, SIDE) * SIDE + lax.rem(here_y + step_y, SIDE)
+
     def ahead(step):
-        return lax.rem(here_x + step // SIDE, SIDE) * SIDE + lax.rem(here_y + step % SIDE, SIDE)
-
-    def behind(step):
-        return lax.rem(here_x - step // SIDE + SIDE, SIDE) * SIDE + lax.rem(
-            here_y - step % SIDE + SIDE, SIDE
-        )
-
-    def offset(turn):
-        step = lax.rem(turn * 5, PEERS)
-        step_x, step_y = step // SIDE, step % SIDE
-        step_x = lax.rem(step_x + core * (SIDE - step_x + SIDE - step_x), SIDE)
-        step_y = lax.rem(step_y + core * (SIDE - step_y + SIDE - step_y), SIDE)
-        return step_x * SIDE + step_y
+        return device(step // SIDE, step % SIDE)
+
+    def along(half, step):
+        return device(0, step) if half else device(step, 0)
+
+    def across(half, step):
+        return device(step, 0) if half else device(0, step)
 
     def around(step):
         return lax.rem(tm + step, TM)
@@ -171,11 +170,12 @@
                 tile = target[f, s]
                 low = jnp.where(tile >= first, jnp.minimum(low, tile), low)
                 high = jnp.where(tile <= last, jnp.maximum(high, tile), high)
-        named[owner * CAP] = low
-        named[owner * CAP + 1] = high
+        names[unit, owner * CAP] = low
+        names[unit, owner * CAP + 1] = high
 
     weights[ENTRIES] = jnp.zeros((TILE, TILE), BF16)
-    stage[SLOTS] = jnp.zeros((TILE, TILE), BF16)
+    for half in range(2):
+        stage[half, SLOTS] = jnp.zeros((HALF, TILE), BF16)
     stats[...] = jnp.zeros_like(stats)
     stim_sum[...] = jnp.zeros_like(stim_sum)
     grad[...] = jnp.zeros_like(grad)
@@ -205,76 +205,13 @@
             )
             mixed[pl.ds(start, LAG), wide] = (both[:LAG] + both[LAG:]).astype(BF16)
 
-    mix_rows(1)
-    take_spikes(3)
-    loads[1].wait()
-    pl.semaphore_wait(barrier, PEERS - 1 + TM - 1)
-
-    halo_copy = pltpu.make_async_remote_copy(
-        src_ref=ext.at[pl.ds(TIME_DEV, LAG)],
-        dst_ref=halo,
-        send_sem=sem_halo.at[0],
-        recv_sem=sem_halo.at[1],
-        device_id=(unit, around(1)),
-        device_id_type=MESH,
-    )
-
-    def names_copy(step):
-        return pltpu.make_async_remote_copy(
-            src_ref=named,
-            dst_ref=names.at[step],
-            send_sem=sem_names.at[0, step],
-            recv_sem=sem_names.at[1, step],
-            device_id=(ahead(step), tm),
-            device_id_type=MESH,
-        )
-
-    def partial_copy(chunk, step, count=1):
-        pair = pl.ds(step * CAP, count * CAP)
-        return pltpu.make_async_remote_copy(
-            src_ref=partial_out.at[chunk, pair],
-            dst_ref=partial_in.at[chunk, pair],
-            send_sem=sem_a_send.at[chunk],
-            recv_sem=sem_a_recv.at[chunk],
-            device_id=(ahead(step), tm),
-            device_id_type=MESH,
-        )
-
-    def resid_copy(chunk, step, count=1):
-        pair = pl.ds(step * CAP, count * CAP)
-        return pltpu.make_async_remote_copy(
-            src_ref=resid_out.at[chunk, pair],
-            dst_ref=resid_in.at[chunk, pair],
-            send_sem=sem_b_send.at[chunk],
-            recv_sem=sem_b_recv.at[chunk],
-            device_id=(behind(step), tm),
-            device_id_type=MESH,
-        )
-
-    @pl.loop(0, CHUNKS)
-    def _(turn):
-        chunk = lax.rem(turn + 1, CHUNKS)
-        start = pl.multiple_of(chunk * LAG, LAG)
-        rows = pl.ds(start, LAG)
-
-        @pl.when(turn == 1)
-        def _():
-            take_spikes(2)
-
-        @pl.when(turn == CHUNKS - 1)
-        def _():
-            halo_copy.wait()
-            ext[pl.ds(0, LAG), :] = halo[...] * jnp.minimum(tm, 1).astype(BF16)
-
-        @pl.when(turn > 0)
-        def _():
-            mix_rows(chunk)
-
-        @pl.loop(1, PEERS + 1)
-        def _(visit):
-            step = offset(visit)
-            owner = ahead(step)
-            low, high = named[owner * CAP], named[owner * CAP + 1]
+    def visit_row(chunk, step_x):
+        rows = pl.ds(pl.multiple_of(chunk * LAG, LAG), LAG)
+
+        @pl.loop(0, SIDE)
+        def _(step_y):
+            owner = device(step_x, step_y)
+            low, high = names[unit, owner * CAP], names[unit, owner * CAP + 1]
 
             def weight_of(s, tile):
                 at = jnp.int32(ENTRIES)
@@ -294,42 +231,154 @@
                 total = total + jnp.dot(
                     mixed[rows, s * TILE : (s + 2) * TILE], block, preferred_element_type=F32
                 )
-            partial_out[chunk, step * CAP] = total[:, :TILE].astype(BF16)
-            partial_out[chunk, step * CAP + 1] = total[:, TILE:].astype(BF16)
-
-            @pl.when(step > 0)
-            def _():
-                partial_copy(chunk, step).start()
-
-                @pl.when(turn == 0)
-                def _():
-                    names_copy(step).start()
+            rounded = total.astype(BF16)
+            for k in range(CAP):
+                piece = rounded[:, k * TILE : (k + 1) * TILE]
+                partial_out[chunk, 0, step_x, step_y, k] = piece[:HALF]
+                partial_out[chunk, 1, step_y, step_x, k] = piece[HALF:]
+
+    order = (1 + 2 * core, 3 - 2 * core, 2)
+    mix_rows(1)
+    loads[1].wait()
+    visit_row(1, order[0])
+    take_spikes(3)
+    pl.semaphore_wait(barrier, PEERS - 1 + TM - 1)
+
+    halo_copy = pltpu.make_async_remote_copy(
+        src_ref=ext.at[pl.ds(TIME_DEV, LAG)],
+        dst_ref=halo,
+        send_sem=sem_halo.at[0],
+        recv_sem=sem_halo.at[1],
+        device_id=(unit, around(1)),
+        device_id_type=MESH,
+    )
+
+    def names_copy(step):
+        return pltpu.make_async_remote_copy(
+            src_ref=names.at[unit],
+            dst_ref=names.at[unit],
+            send_sem=sem_names.at[0, step],
+            recv_sem=sem_names.at[1, step],
+            device_id=(ahead(step), tm),
+            device_id_type=MESH,
+        )
+
+    def copy(source, place, kind, chunk, receiver):
+        return pltpu.make_async_remote_copy(
+            src_ref=source,
+            dst_ref=place,
+            send_sem=sem_send.at[kind],
+            recv_sem=sem_recv.at[kind, chunk],
+            device_id=(receiver, tm),
+            device_id_type=MESH,
+        )
+
+    def arrived(place, kind, chunk):
+        copy(place, place, kind, chunk, along(0, 1)).wait_recv()
+
+    def lower(half_ref):
+        return half_ref.at[pl.ds(0, TILES_DEV // 2)]
+
+    def upper(half_ref):
+        return half_ref.at[pl.ds(TILES_DEV // 2, TILES_DEV // 2)]
+
+    def send_partials(turn, chunk):
+        @pl.when(turn == 1)
+        def _():
+            take_spikes(2)
+
+        @pl.when(turn == CHUNKS - 1)
+        def _():
+            halo_copy.wait()
+            ext[pl.ds(0, LAG), :] = halo[...] * jnp.minimum(tm, 1).astype(BF16)
+
+        @pl.when(turn > 0)
+        def _():
+            mix_rows(chunk)
+            visit_row(chunk, order[0])
+
+        def send(half, step):
+            copy(
+                partial_out.at[chunk, half, step],
+                partial_in.at[chunk, half, step],
+                0,
+                chunk,
+                along(half, step),
+            ).start()
+
+        send(0, order[0])
+        for step in order[1:]:
+            visit_row(chunk, step)
+            send(0, step)
+        visit_row(chunk, 0)
+        for step in order:
+            send(1, step)
 
         @pl.when(turn == 0)
         def _():
+            @pl.loop(1, PEERS)
+            def _(step):
+                names_copy(step).start()
+
             halo_copy.start()
 
-    @pl.loop(1, PEERS)
-    def _(step):
-        names_copy(step).wait()
-
-    for k in range(CAP * PEERS):
-        names[0, k] = named[k]
-    for load in loads[2:]:
-        load.wait()
-
-    @pl.loop(0, CHUNKS)
-    def _(turn):
-        chunk = lax.rem(turn + 1, CHUNKS)
+    def add_sources(chunk):
+        arrived(partial_in.at[chunk, :, pl.ds(1, SIDE - 1)], 0, chunk)
+        for half in range(2):
+            stage[half, : SLOTS // SIDE] = partial_out[chunk, half, 0].reshape(
+                SLOTS // SIDE, HALF, TILE
+            )
+            stage[half, SLOTS // SIDE : SLOTS] = partial_in[chunk, half, 1:].reshape(
+                SLOTS - SLOTS // SIDE, HALF, TILE
+            )
+
+            @pl.loop(0, SIDE)
+            def _(step):
+                owner = across(half, step)
+
+                @pl.loop(0, TILES_DEV)
+                def _(local):
+                    tile = owner * TILES_DEV + local
+                    total = jnp.zeros((HALF, TILE), F32)
+                    for back in range(SIDE):
+                        source = along(half, (SIDE - back) % SIDE)
+                        first = back * (SIDE * CAP) + step * CAP
+                        at = jnp.where(
+                            names[source, owner * CAP] == tile,
+                            first,
+                            jnp.where(names[source, owner * CAP + 1] == tile, first + 1, SLOTS),
+                        )
+                        total = total + stage[half, at].astype(F32)
+                    dense[chunk, half, step, local] = total.astype(BF16)
+
+            far = dense.at[chunk, half, 2]
+            copy(lower(far), far_in.at[chunk, half, 0], 1, chunk, across(half, 1)).start()
+            copy(upper(far), far_in.at[chunk, half, 1], 1, chunk, across(half, 3)).start()
+
+    def pass_sums(chunk):
+        arrived(far_in.at[chunk], 1, chunk)
+        middle = TILES_DEV // 2
+        for half in range(2):
+            dense[chunk, half, 1, :middle] = (
+                dense[chunk, half, 1, :middle].astype(F32) + far_in[chunk, half, 0].astype(F32)
+            ).astype(BF16)
+            dense[chunk, half, 3, middle:] = (
+                dense[chunk, half, 3, middle:].astype(F32) + far_in[chunk, half, 1].astype(F32)
+            ).astype(BF16)
+            for place, step in ((0, 1), (1, 3)):
+                copy(
+                    dense.at[chunk, half, step],
+                    near_in.at[chunk, half, place],
+                    2,
+                    chunk,
+                    across(half, step),
+                ).start()
+
+    def make_resid(chunk):
         start = pl.multiple_of(chunk * LAG, LAG)
         rows = pl.ds(start, LAG)
         spike_rows = pl.ds(pl.multiple_of(start + LAG, LAG), LAG)
-
-        for k in range(CAP):
-            stage[k] = partial_out[chunk, k]
-
-        partial_copy(chunk, 1, PEERS - 1).wait_recv()
-        stage[CAP:SLOTS] = partial_in[chunk, CAP:]
+        arrived(near_in.at[chunk], 2, chunk)
 
         @pl.loop(0, UNITS_DEV // WIDE)
         def _(part):
@@ -341,46 +390,42 @@
             drive = bias[:, wide] + lax.dot_general(
                 stim[:, rows], filt[:, wide], (((0,), (0,)), ((), ())), preferred_element_type=F32
             )
-            for half in range(2):
-                inner = slice(half * TILE, (half + 1) * TILE)
-                cols = pl.ds(pl.multiple_of(left + half * TILE, TILE), TILE)
-                tile = unit * TILES_DEV + part * 2 + half
-
+            for side in range(2):
+                inner = slice(side * TILE, (side + 1) * TILE)
+                cols = pl.ds(pl.multiple_of(left + side * TILE, TILE), TILE)
+                tile = part * 2 + side
                 logit = drive[:, inner]
                 for b in range(NB):
                     h = hist[b * LAG : (b + 1) * LAG, inner]
                     logit = logit + hist_weight[b : b + 1, cols] * h
-                coupling = jnp.zeros((LAG, TILE), F32)
-                for step in range(PEERS):
-                    first = names[step, unit * CAP]
-                    second = names[step, unit * CAP + 1]
-                    at = jnp.where(
-                        first == tile,
-                        step * CAP,
-                        jnp.where(second == tile, step * CAP + 1, SLOTS),
-                    )
-                    coupling = coupling + stage[at].astype(F32)
+                coupling = jnp.concatenate(
+                    [
+                        dense[chunk, half, 0, tile].astype(F32)
+                        + near_in[chunk, half, 0, tile].astype(F32)
+                        + near_in[chunk, half, 1, tile].astype(F32)
+                        for half in range(2)
+                    ],
+                    axis=0,
+                )
                 resid = ext[spike_rows, cols].astype(F32) - jnp.exp(logit + coupling)
                 rounded = resid.astype(BF16)
-                resid_tiles[part * 2 + half] = rounded
+                for half in range(2):
+                    resid_out[chunk, half, tile] = rounded[half * HALF : (half + 1) * HALF]
                 resid_rows[:, cols] = rounded
                 stats[NB : NB + 1, cols] += jnp.sum(resid, axis=0, keepdims=True)
                 for b in range(NB):
                     h = hist[b * LAG : (b + 1) * LAG, inner]
                     stats[b : b + 1, cols] += jnp.sum(h * resid, axis=0, keepdims=True)
 
-        @pl.loop(1, PEERS + 1)
-        def _(visit):
-            step = offset(visit)
-            for k in range(CAP):
-                tile = names[step, unit * CAP + k] - unit * TILES_DEV
-                tile = jnp.minimum(jnp.maximum(tile, 0), TILES_DEV - 1)
-                resid_out[chunk, step * CAP + k] = resid_tiles[tile]
-
-            @pl.when(step > 0)
-            def _():
-                resid_copy(chunk, step).start()
-
+        for step, place in ((1, 1), (3, 0)):
+            for half in range(2):
+                copy(
+                    resid_out.at[chunk, half],
+                    got.at[chunk, half, place],
+                    3,
+                    chunk,
+                    across(half, step),
+                ).start()
         for block in range(TM):
             stim_sum[block] += lax.dot_general(
                 stim[:, rows],
@@ -388,6 +433,77 @@
                 (((1,), (0,)), ((), ())),
                 preferred_element_type=F32,
             )
+
+    def forward_resid(chunk):
+        arrived(got.at[chunk, :, pl.ds(0, 2)], 3, chunk)
+        for half in range(2):
+            far = got.at[chunk, half, 2]
+            copy(
+                lower(got.at[chunk, half, 1]), lower(far), 4, chunk, across(half, 1)
+            ).start()
+            copy(
+                upper(got.at[chunk, half, 0]), upper(far), 4, chunk, across(half, 3)
+            ).start()
+
+    def send_named(chunk):
+        arrived(got.at[chunk, :, 2], 4, chunk)
+        for half in range(2):
+            stage[half, :TILES_DEV] = resid_out[chunk, half]
+            for step, place in ((1, 0), (2, 2), (3, 1)):
+                stage[half, step * TILES_DEV : (step + 1) * TILES_DEV] = got[chunk, half, place]
+            for receiver in (1, 3, 2, 0):
+
+                @pl.loop(0, SIDE)
+                def _(step):
+                    owner = across(half, step)
+                    for k in range(CAP):
+                        local = (
+                            names[along(half, receiver), owner * CAP + k] - owner * TILES_DEV
+                        )
+                        local = jnp.minimum(jnp.maximum(local, 0), TILES_DEV - 1)
+                        pick[chunk, half, receiver, step, k] = stage[
+                            half, step * TILES_DEV + local
+                        ]
+
+                if receiver:
+                    copy(
+                        pick.at[chunk, half, receiver],
+                        resid_in.at[chunk, half, receiver],
+                        5,
+                        chunk,
+                        along(half, receiver),
+                    ).start()
+
+    def take_resid(chunk):
+        arrived(resid_in.at[chunk, :, pl.ds(1, SIDE - 1)], 5, chunk)
+        for half in range(2):
+            stage[half, : SLOTS // SIDE] = pick[chunk, half, 0].reshape(SLOTS // SIDE, HALF, TILE)
+            stage[half, SLOTS // SIDE : SLOTS] = resid_in[chunk, half, 1:].reshape(
+                SLOTS - SLOTS // SIDE, HALF, TILE
+            )
+
+    def chosen_tile(s, f):
+        owner = target[f, s] // TILES_DEV
+        gone_x = lax.rem(owner // SIDE - here_x + SIDE, SIDE)
+        gone_y = lax.rem(owner % SIDE - here_y + SIDE, SIDE)
+        back_x = lax.rem(SIDE - gone_x, SIDE)
+        back_y = lax.rem(SIDE - gone_y, SIDE)
+        rank = (target[f, s] == names[unit, owner * CAP + 1]).astype(jnp.int32)
+        return jnp.concatenate(
+            [
+                stage[0, (back_x * SIDE + gone_y) * CAP + rank],
+                stage[1, (back_y * SIDE + gone_x) * CAP + rank],
+            ],
+            axis=0,
+        )
+
+    def add_grad(chunk, s):
+        grad[s] += lax.dot_general(
+            mixed[pl.ds(pl.multiple_of(chunk * LAG, LAG), LAG), s * TILE : (s + 1) * TILE],
+            jnp.concatenate([chosen_tile(s, f) for f in range(FAN)], axis=1),
+            (((0,), (0,)), ((), ())),
+            preferred_element_type=F32,
+        )
 
     def stats_copy(step):
         return pltpu.make_async_remote_copy(
@@ -420,39 +536,46 @@
             device_id_type=MESH,
         ).wait()
 
-    @pl.loop(1, TM)
-    def _(step):
-        stats_copy(step).start()
-        stim_copy(step).start()
-
-    def slot_of(s, f):
-        owner = target[f, s] // TILES_DEV
-        step_x = lax.rem(owner // SIDE - here_x + SIDE, SIDE)
-        step_y = lax.rem(owner % SIDE - here_y + SIDE, SIDE)
-        rank = (target[f, s] == named[owner * CAP + 1]).astype(jnp.int32)
-        return (step_x * SIDE + step_y) * CAP + rank
-
-    def take_resid(chunk):
-        for k in range(CAP):
-            stage[k] = resid_out[chunk, k]
-        partial_copy(chunk, 1, PEERS - 1).wait_send()
-        resid_copy(chunk, 1, PEERS - 1).wait_recv()
-        stage[CAP:SLOTS] = resid_in[chunk, CAP:]
-
-    def add_grad(chunk, s):
-        chosen = jnp.concatenate([stage[slot_of(s, f)] for f in range(FAN)], axis=1)
-        grad[s] += lax.dot_general(
-            mixed[pl.ds(pl.multiple_of(chunk * LAG, LAG), LAG), s * TILE : (s + 1) * TILE],
-            chosen,
-            (((0,), (0,)), ((), ())),
-            preferred_element_type=F32,
-        )
-
-    @pl.loop(1, CHUNKS)
-    def _(chunk):
-        take_resid(chunk)
-        for s in range(TILES_DEV):
-            add_grad(chunk, s)
+    last = CHUNKS - 1
+
+    def during(turn, delay, step):
+        @pl.when((turn >= delay) & (turn < delay + CHUNKS))
+        def _():
+            step(lax.rem(turn - delay + 1, CHUNKS))
+
+    @pl.loop(0, 6 + CHUNKS)
+    def _(turn):
+        during(turn, 0, functools.partial(send_partials, turn))
+
+        @pl.when(turn == 2)
+        def _():
+            @pl.loop(1, PEERS)
+            def _(step):
+                names_copy(step).wait()
+
+            for load in loads[2:]:
+                load.wait()
+
+        during(turn, 2, add_sources)
+        during(turn, 3, pass_sums)
+        during(turn, 4, make_resid)
+
+        @pl.when(turn == 4 + last)
+        def _():
+            @pl.loop(1, TM)
+            def _(step):
+                stats_copy(step).start()
+                stim_copy(step).start()
+
+        during(turn, 5, forward_resid)
+        during(turn, 6, send_named)
+
+        @pl.when(turn >= 7)
+        def _():
+            chunk = lax.rem(turn - 7 + 1, CHUNKS)
+            take_resid(chunk)
+            for s in range(TILES_DEV):
+                add_grad(chunk, s)
 
     share = TILE // TM
     half_tiles = TILES_DEV // 2
@@ -511,9 +634,18 @@
         stim_total = stim_total + stim_in[step]
     out_stim[...] = stim_total
 
-    for chunk in range(CHUNKS):
-        resid_copy(chunk, 1, PEERS - 1).wait_send()
-
+    others = pl.ds(1, SIDE - 1)
+    for kind, place in enumerate(
+        (
+            partial_in.at[:, :, others],
+            far_in,
+            near_in,
+            got.at[:, :, pl.ds(0, 2)],
+            got.at[:, :, 2],
+            resid_in.at[:, :, others],
+        )
+    ):
+        copy(place, place, kind, 0, along(0, 1)).wait_send()
     for half in range(2):
         for z in range(SIDE):
             pair_copy(half, z).wait_send()
@@ -565,14 +697,17 @@
             pltpu.VMEM((ENTRIES + 1, TILE, TILE), BF16),
             pltpu.VMEM((NB * LAG, WIDE), F32),
             pltpu.VMEM((TIME_DEV, UNITS_DEV), BF16),
-            pltpu.VMEM((CHUNKS, SLOTS, LAG, TILE), BF16),
-            pltpu.VMEM((CHUNKS, SLOTS, LAG, TILE), BF16),
-            pltpu.VMEM((SLOTS + 1, LAG, TILE), BF16),
-            pltpu.VMEM((TILES_DEV, LAG, TILE), BF16),
+            pltpu.VMEM((CHUNKS, 2, SIDE, SIDE, CAP, HALF, TILE), BF16),
+            pltpu.VMEM((CHUNKS, 2, SIDE, SIDE, CAP, HALF, TILE), BF16),
+            pltpu.VMEM((CHUNKS, 2, SIDE, TILES_DEV, HALF, TILE), BF16),
+            pltpu.VMEM((CHUNKS, 2, 2, TILES_DEV // 2, HALF, TILE), BF16),
+            pltpu.VMEM((CHUNKS, 2, 2, TILES_DEV, HALF, TILE), BF16),
+            pltpu.VMEM((2, SLOTS + 1, HALF, TILE), BF16),
             pltpu.VMEM((LAG, UNITS_DEV), BF16),
-            pltpu.VMEM((CHUNKS, SLOTS, LAG, TILE), BF16),
-            pltpu.VMEM((CHUNKS, SLOTS, LAG, TILE), BF16),
-            pltpu.SMEM((SLOTS,), jnp.int32),
+            pltpu.VMEM((CHUNKS, 2, TILES_DEV, HALF, TILE), BF16),
+            pltpu.VMEM((CHUNKS, 2, SIDE - 1, TILES_DEV, HALF, TILE), BF16),
+            pltpu.VMEM((CHUNKS, 2, SIDE, SIDE, CAP, HALF, TILE), BF16),
+            pltpu.VMEM((CHUNKS, 2, SIDE, SIDE, CAP, HALF, TILE), BF16),
             pltpu.SMEM((PEERS, SLOTS), jnp.int32),
             pltpu.VMEM((TILES_DEV, TILE, FAN * TILE), F32),
             pltpu.VMEM((16, UNITS_DEV), F32),
@@ -587,10 +722,8 @@
             dma((CHUNKS,)),
             dma((2,)),
             dma((2, PEERS)),
-            dma((CHUNKS,)),
-            dma((CHUNKS,)),
-            dma((CHUNKS,)),
-            dma((CHUNKS,)),
+            dma((6,)),
+            dma((6, CHUNKS)),
             dma((2,)),
             dma((2,)),
             dma((2, 2, SIDE)),

time: 118 us -> 110 us (0.932)
  Pallas kernels: 117 us -> 110 us
    pallas_call x1, Pallas kernels: 115 us -> 108 us  [shards(): pl.pallas_call(main_kernel, out_shape=[jax.ShapeDtypeStruct((16, UNITS_DE...]
where the time goes in v5:
time: 110 us
  Pallas kernels  110 us (100%)
    pallas_call x1, Pallas kernels, shards(): pl.pallas_call(main_kernel, out_shape=[jax.ShapeDtypeStruct((16, UNITS_DE...  108 us

profile of v5, /device:TPU:1, one launch (start us, length us, event | category | flops | bytes accessed | tf_op | source)
XLA Modules:
  0.0 110.2 jit_solution(14107498821832817837)
XLA Ops:
  0.6 107.8 %shard_map.120 = (f32[16,1024]{1,0:T(8,128)}, f32[64,128]{1,0:T(8,128)}, f32[8,16,512]{2,1,0:T(8,128)}) custom-call(s32[4,8]{1,0:T(4,128)} %bitcast.11, f32[10]{0:T(128)} %mix.1, s32[512,1024]{1,0:T(8,128)} %spikes_hbm.1, bf16[64,512]{1,0:T(8,128)(2,1)} %bitcast.9, f32[1,1024]{1,0:T(1,128)} %bitcast.10, f32[10,1024]{1,0:T(8,128)} %hist_weight_hbm.1, ...), custom_call_target="tpu_custom_call" | custom-call | tf_op jit(solution)/shard_map/pallas_call | solution.py:678
  108.4 1.8 %shard_map.121 = (f32[1,1024]{1,0:T(1,128)}, f32[10,1024]{1,0:T(8,128)}, f32[64,128]{1,0:T(8,128)}, f32[8,4,16,128]{3,2,1,0:T(8,128)}) custom-call(f32[16,1024]{1,0:T(8,128)} %get-tuple-element.11.stats, f32[64,128]{1,0:T(8,128)} %get-tuple-element.12.stim, f32[8,16,512]{2,1,0:T(8,128)} %get-tuple-element.13.coupling), custom_call_target="tpu_custom_call" | custom-call | tf_op jit(solution)/shard_map/pallas_call | solution.py:746

commit v6 on v5

--- a/solution.py
+++ b/solution.py
@@ -90,6 +90,7 @@
     stim_in,
     pair_in,
     pair_out,
+    zed_far,
     zed_in,
     final,
     sem_load,
@@ -101,6 +102,7 @@
     sem_stats,
     sem_stim,
     sem_pair,
+    sem_far,
     sem_zed,
 ):
     unit = lax.axis_index("unit")
@@ -111,9 +113,6 @@
     def device(step_x, step_y):
         return lax.rem(here_x + step_x, SIDE) * SIDE + lax.rem(here_y + step_y, SIDE)
 
-    def ahead(step):
-        return device(step // SIDE, step % SIDE)
-
     def along(half, step):
         return device(0, step) if half else device(step, 0)
 
@@ -125,9 +124,11 @@
 
     barrier = pltpu.get_barrier_semaphore()
 
-    @pl.loop(1, PEERS)
-    def _(step):
-        pl.semaphore_signal(barrier, inc=1, device_id=(ahead(step), tm), device_id_type=MESH)
+    for step in range(1, SIDE):
+        for half in range(2):
+            pl.semaphore_signal(
+                barrier, inc=1, device_id=(along(half, step), tm), device_id_type=MESH
+            )
 
     @pl.loop(1, TM)
     def _(step):
@@ -205,11 +206,12 @@
             )
             mixed[pl.ds(start, LAG), wide] = (both[:LAG] + both[LAG:]).astype(BF16)
 
-    def visit_row(chunk, step_x):
+    def visit(chunk, count, steps):
         rows = pl.ds(pl.multiple_of(chunk * LAG, LAG), LAG)
 
-        @pl.loop(0, SIDE)
-        def _(step_y):
+        @pl.loop(0, count)
+        def _(turn):
+            step_x, step_y = steps(turn)
             owner = device(step_x, step_y)
             low, high = names[unit, owner * CAP], names[unit, owner * CAP + 1]
 
@@ -238,11 +240,16 @@
                 partial_out[chunk, 1, step_y, step_x, k] = piece[HALF:]
 
     order = (1 + 2 * core, 3 - 2 * core, 2)
+
+    def visit_first(chunk):
+        visit(chunk, SIDE, lambda turn: (order[0], turn))
+        visit(chunk, 3, lambda turn: (2 * turn - turn // 2 * order[0], order[0]))
+
     mix_rows(1)
     loads[1].wait()
-    visit_row(1, order[0])
+    visit_first(1)
     take_spikes(3)
-    pl.semaphore_wait(barrier, PEERS - 1 + TM - 1)
+    pl.semaphore_wait(barrier, 2 * (SIDE - 1) + TM - 1)
 
     halo_copy = pltpu.make_async_remote_copy(
         src_ref=ext.at[pl.ds(TIME_DEV, LAG)],
@@ -253,13 +260,13 @@
         device_id_type=MESH,
     )
 
-    def names_copy(step):
+    def names_copy(half, step):
         return pltpu.make_async_remote_copy(
             src_ref=names.at[unit],
             dst_ref=names.at[unit],
-            send_sem=sem_names.at[0, step],
-            recv_sem=sem_names.at[1, step],
-            device_id=(ahead(step), tm),
+            send_sem=sem_names.at[0, half, step],
+            recv_sem=sem_names.at[1, half, step],
+            device_id=(along(half, step), tm),
             device_id_type=MESH,
         )
 
@@ -295,7 +302,7 @@
         @pl.when(turn > 0)
         def _():
             mix_rows(chunk)
-            visit_row(chunk, order[0])
+            visit_first(chunk)
 
         def send(half, step):
             copy(
@@ -307,18 +314,22 @@
             ).start()
 
         send(0, order[0])
-        for step in order[1:]:
-            visit_row(chunk, step)
-            send(0, step)
-        visit_row(chunk, 0)
-        for step in order:
-            send(1, step)
+        send(1, order[0])
+        visit(chunk, 3, lambda turn: (order[1], 2 * turn - turn // 2 * order[0]))
+        send(0, order[1])
+        visit(chunk, 2, lambda turn: (2 * turn, order[1]))
+        send(1, order[1])
+        visit(chunk, 2, lambda turn: (order[2], 2 * turn))
+        send(0, order[2])
+        visit(chunk, 1, lambda turn: (0, order[2]))
+        send(1, order[2])
+        visit(chunk, 1, lambda turn: (0, 0))
 
         @pl.when(turn == 0)
         def _():
-            @pl.loop(1, PEERS)
-            def _(step):
-                names_copy(step).start()
+            for half in range(2):
+                for step in range(1, SIDE):
+                    names_copy(half, step).start()
 
             halo_copy.start()
 
@@ -543,15 +554,15 @@
         def _():
             step(lax.rem(turn - delay + 1, CHUNKS))
 
-    @pl.loop(0, 6 + CHUNKS)
+    @pl.loop(0, 7 + CHUNKS)
     def _(turn):
         during(turn, 0, functools.partial(send_partials, turn))
 
         @pl.when(turn == 2)
         def _():
-            @pl.loop(1, PEERS)
-            def _(step):
-                names_copy(step).wait()
+            for half in range(2):
+                for step in range(1, SIDE):
+                    names_copy(half, step).wait()
 
             for load in loads[2:]:
                 load.wait()
@@ -570,9 +581,9 @@
         during(turn, 5, forward_resid)
         during(turn, 6, send_named)
 
-        @pl.when(turn >= 7)
+        @pl.when(turn >= 8)
         def _():
-            chunk = lax.rem(turn - 7 + 1, CHUNKS)
+            chunk = lax.rem(turn - 8 + 1, CHUNKS)
             take_resid(chunk)
             for s in range(TILES_DEV):
                 add_grad(chunk, s)
@@ -591,14 +602,26 @@
             device_id_type=MESH,
         )
 
-    def zed_copy(half, step):
-        z = lax.rem(here_z + step, SIDE)
+    forth, back = lax.rem(here_z + 1, SIDE), lax.rem(here_z + 3, SIDE)
+    ways = (forth, back)
+
+    def far_copy(half):
         return pltpu.make_async_remote_copy(
-            src_ref=pair_out.at[half, z],
-            dst_ref=zed_in.at[half, step],
-            send_sem=sem_zed.at[0, half, step],
-            recv_sem=sem_zed.at[1, half, step],
-            device_id=(unit, z * 2 + core),
+            src_ref=pair_out.at[half, lax.rem(here_z + 2, SIDE)],
+            dst_ref=zed_far.at[half],
+            send_sem=sem_far.at[0, half],
+            recv_sem=sem_far.at[1, half],
+            device_id=(unit, ways[half] * 2 + core),
+            device_id_type=MESH,
+        )
+
+    def zed_copy(half, way):
+        return pltpu.make_async_remote_copy(
+            src_ref=pair_out.at[half, ways[way]],
+            dst_ref=zed_in.at[half, way],
+            send_sem=sem_zed.at[0, half, way],
+            recv_sem=sem_zed.at[1, half, way],
+            device_id=(unit, ways[way] * 2 + core),
             device_id_type=MESH,
         )
 
@@ -610,14 +633,21 @@
     for half in range(2):
         for s in range(half * half_tiles, (half + 1) * half_tiles):
             add_grad(0, s)
-        for step in (2, 1, 3, 0):
+        for step in (2, 3 - 2 * half, 1 + 2 * half, 0):
             pair_copy(half, lax.rem(here_z + step, SIDE)).start()
     for half in range(2):
-        for step in (2, 1, 3):
-            z = lax.rem(here_z + step, SIDE)
+        for z in (lax.rem(here_z + 2, SIDE), ways[1 - half]):
             pair_copy(half, z).wait_recv()
-            pair_out[half, z] = both(half, z).astype(pair_out.dtype)
-            zed_copy(half, step).start()
+            pair_out[half, z] = both(half, z).astype(BF16)
+        far_copy(half).start()
+        zed_copy(half, 1 - half).start()
+    for half in range(2):
+        z = ways[half]
+        pair_copy(half, z).wait_recv()
+        own = both(half, z)
+        far_copy(half).wait_recv()
+        pair_out[half, z] = (own + zed_far[half].astype(F32)).astype(BF16)
+        zed_copy(half, half).start()
     for half in range(2):
         pair_copy(half, here_z).wait_recv()
         final[half * half_tiles : (half + 1) * half_tiles] = both(half, here_z)
@@ -652,9 +682,10 @@
     for half in range(2):
         tiles = slice(half * half_tiles, (half + 1) * half_tiles)
         total = final[tiles]
-        for step in (1, 2, 3):
-            zed_copy(half, step).wait()
-            total = total + zed_in[half, step].astype(F32)
+        far_copy(half).wait_send()
+        for way in range(2):
+            zed_copy(half, way).wait()
+            total = total + zed_in[half, way].astype(F32)
         out_coupling[tiles] = total
 
 
@@ -716,18 +747,20 @@
             pltpu.VMEM((TM, STIM, TILE), F32),
             pltpu.VMEM((2, SIDE, TILES_DEV // 2, share, FAN * TILE), F32),
             pltpu.VMEM((2, SIDE, TILES_DEV // 2, share, FAN * TILE), BF16),
-            pltpu.VMEM((2, SIDE, TILES_DEV // 2, share, FAN * TILE), BF16),
+            pltpu.VMEM((2, TILES_DEV // 2, share, FAN * TILE), BF16),
+            pltpu.VMEM((2, 2, TILES_DEV // 2, share, FAN * TILE), BF16),
             pltpu.VMEM((TILES_DEV, share, FAN * TILE), F32),
             dma((6,)),
             dma((CHUNKS,)),
             dma((2,)),
-            dma((2, PEERS)),
+            dma((2, 2, SIDE)),
             dma((6,)),
             dma((6, CHUNKS)),
             dma((2,)),
             dma((2,)),
             dma((2, 2, SIDE)),
-            dma((2, 2, SIDE)),
+            dma((2, 2)),
+            dma((2, 2, 2)),
         ],
         compiler_params=pltpu.CompilerParams(
             collective_id=0, has_side_effects=True, vmem_limit_bytes=56 * 1024 * 1024

time: 110 us -> 108 us (0.982)
  Pallas kernels: 110 us -> 107 us
    pallas_call x1, Pallas kernels: 108 us -> 105 us  [shards(): pl.pallas_call(main_kernel, out_shape=[jax.ShapeDtypeStruct((16, UNITS_DE...]
where the time goes in v6:
time: 108 us
  Pallas kernels  107 us (99%)
    pallas_call x1, Pallas kernels, shards(): pl.pallas_call(main_kernel, out_shape=[jax.ShapeDtypeStruct((16, UNITS_DE...  105 us

profile of v6, /device:TPU:1, one launch (start us, length us, event | category | flops | bytes accessed | tf_op | source)
XLA Modules:
  0.0 107.6 jit_solution(9999816596176953402)
XLA Ops:
  0.6 105.2 %shard_map.120 = (f32[16,1024]{1,0:T(8,128)}, f32[64,128]{1,0:T(8,128)}, f32[8,16,512]{2,1,0:T(8,128)}) custom-call(s32[4,8]{1,0:T(4,128)} %bitcast.11, f32[10]{0:T(128)} %mix.1, s32[512,1024]{1,0:T(8,128)} %spikes_hbm.1, bf16[64,512]{1,0:T(8,128)(2,1)} %bitcast.9, f32[1,1024]{1,0:T(1,128)} %bitcast.10, f32[10,1024]{1,0:T(8,128)} %hist_weight_hbm.1, ...), custom_call_target="tpu_custom_call" | custom-call | tf_op jit(solution)/shard_map/pallas_call | solution.py:709
  105.8 1.8 %shard_map.121 = (f32[1,1024]{1,0:T(1,128)}, f32[10,1024]{1,0:T(8,128)}, f32[64,128]{1,0:T(8,128)}, f32[8,4,16,128]{3,2,1,0:T(8,128)}) custom-call(f32[16,1024]{1,0:T(8,128)} %get-tuple-element.11.stats, f32[64,128]{1,0:T(8,128)} %get-tuple-element.12.stim, f32[8,16,512]{2,1,0:T(8,128)} %get-tuple-element.13.coupling), custom_call_target="tpu_custom_call" | custom-call | tf_op jit(solution)/shard_map/pallas_call | solution.py:779

commit v7 on v6

--- a/solution.py
+++ b/solution.py
@@ -462,7 +462,7 @@
             stage[half, :TILES_DEV] = resid_out[chunk, half]
             for step, place in ((1, 0), (2, 2), (3, 1)):
                 stage[half, step * TILES_DEV : (step + 1) * TILES_DEV] = got[chunk, half, place]
-            for receiver in (1, 3, 2, 0):
+            for receiver in (2, 1, 3, 0):
 
                 @pl.loop(0, SIDE)
                 def _(step):
@@ -554,11 +554,11 @@
         def _():
             step(lax.rem(turn - delay + 1, CHUNKS))
 
-    @pl.loop(0, 7 + CHUNKS)
+    @pl.loop(0, 10)
     def _(turn):
         during(turn, 0, functools.partial(send_partials, turn))
 
-        @pl.when(turn == 2)
+        @pl.when(turn == 1)
         def _():
             for half in range(2):
                 for step in range(1, SIDE):
@@ -567,23 +567,26 @@
             for load in loads[2:]:
                 load.wait()
 
-        during(turn, 2, add_sources)
-        during(turn, 3, pass_sums)
-        during(turn, 4, make_resid)
-
-        @pl.when(turn == 4 + last)
+        during(turn, 1, add_sources)
+
+        during(turn, 2, pass_sums)
+
+        during(turn, 3, make_resid)
+
+        @pl.when(turn == 3 + last)
         def _():
             @pl.loop(1, TM)
             def _(step):
                 stats_copy(step).start()
                 stim_copy(step).start()
 
-        during(turn, 5, forward_resid)
-        during(turn, 6, send_named)
-
-        @pl.when(turn >= 8)
+        during(turn, 4, forward_resid)
+
+        during(turn, 5, send_named)
+
+        @pl.when(turn >= 7)
         def _():
-            chunk = lax.rem(turn - 8 + 1, CHUNKS)
+            chunk = lax.rem(turn - 7 + 1, CHUNKS)
             take_resid(chunk)
             for s in range(TILES_DEV):
                 add_grad(chunk, s)
@@ -709,9 +712,9 @@
     sums = pl.pallas_call(
         main_kernel,
         out_shape=[
-            jax.ShapeDtypeStruct((16, UNITS_DEV), F32),
-            jax.ShapeDtypeStruct((STIM, TILE), F32),
-            jax.ShapeDtypeStruct((TILES_DEV, share, FAN * TILE), F32),
+            pltpu.VMEM((16, UNITS_DEV), F32),
+            pltpu.VMEM((STIM, TILE), F32),
+            pltpu.VMEM((TILES_DEV, share, FAN * TILE), F32),
         ],
         in_specs=[smem] * 2 + [anywhere] * 7,
         out_specs=[vmem] * 3,
@@ -786,7 +789,7 @@
         ],
         in_specs=[vmem] * 3,
         out_specs=[vmem] * 4,
-    )(*sums)
+    )(*[pltpu.with_memory_space_constraint(total, pltpu.VMEM) for total in sums])
     return (grad_bias.reshape(UNITS_DEV), grad_hist, grad_stim.T, grad_coupling)
 
 

time: 108 us -> 106 us (0.981)
  Pallas kernels: 107 us -> 105 us
    pallas_call x1, Pallas kernels: 105 us -> 104 us  [shards(): pl.pallas_call(main_kernel, out_shape=[pltpu.VMEM((16, UNITS_DEV), F32),...]
where the time goes in v7:
time: 106 us; the launch traced here: 105 us
  Pallas kernels  105 us (99%)
    pallas_call x1, Pallas kernels, shards(): pl.pallas_call(main_kernel, out_shape=[pltpu.VMEM((16, UNITS_DEV), F32),...  104 us

profile of v7, /device:TPU:1, one launch (start us, length us, event | category | flops | bytes accessed | tf_op | source)
XLA Modules:
  0.0 105.4 jit_solution(13610962824230001234)
XLA Ops:
  0.6 104.0 %shard_map.120 = (f32[16,1024]{1,0:T(8,128)S(1)}, f32[64,128]{1,0:T(8,128)S(1)}, f32[8,16,512]{2,1,0:T(8,128)S(1)}) custom-call(s32[4,8]{1,0:T(4,128)} %bitcast.11, f32[10]{0:T(128)} %mix.1, s32[512,1024]{1,0:T(8,128)} %spikes_hbm.1, bf16[64,512]{1,0:T(8,128)(2,1)} %bitcast.9, f32[1,1024]{1,0:T(1,128)} %bitcast.10, f32[10,1024]{1,0:T(8,128)} %hist_weight_hbm.1, ...), custom_call_target="tpu_custom_call" | custom-call | tf_op jit(solution)/shard_map/pallas_call | solution.py:712
  104.7 0.8 shard_map.121

commit v8 on v7

--- a/solution.py
+++ b/solution.py
@@ -88,6 +88,7 @@
     stats_in,
     stim_sum,
     stim_in,
+    pair_give,
     pair_in,
     pair_out,
     zed_far,
@@ -595,9 +596,8 @@
     half_tiles = TILES_DEV // 2
 
     def pair_copy(half, z):
-        given = pl.ds(pl.multiple_of((z * 2 + 1 - core) * share, share), share)
         return pltpu.make_async_remote_copy(
-            src_ref=grad.at[pl.ds(half * half_tiles, half_tiles), given],
+            src_ref=pair_give.at[half, z],
             dst_ref=pair_in.at[half, z],
             send_sem=sem_pair.at[0, half, z],
             recv_sem=sem_pair.at[1, half, z],
@@ -630,14 +630,19 @@
 
     def both(half, z):
         kept = pl.ds(pl.multiple_of((z * 2 + core) * share, share), share)
-        return grad[half * half_tiles : (half + 1) * half_tiles, kept, :] + pair_in[half, z]
+        return grad[half * half_tiles : (half + 1) * half_tiles, kept, :] + pair_in[half, z].astype(F32)
 
     take_resid(0)
     for half in range(2):
         for s in range(half * half_tiles, (half + 1) * half_tiles):
             add_grad(0, s)
         for step in (2, 3 - 2 * half, 1 + 2 * half, 0):
-            pair_copy(half, lax.rem(here_z + step, SIDE)).start()
+            z = lax.rem(here_z + step, SIDE)
+            given = pl.ds(pl.multiple_of((z * 2 + 1 - core) * share, share), share)
+            pair_give[half, z] = grad[
+                half * half_tiles : (half + 1) * half_tiles, given, :
+            ].astype(BF16)
+            pair_copy(half, z).start()
     for half in range(2):
         for z in (lax.rem(here_z + 2, SIDE), ways[1 - half]):
             pair_copy(half, z).wait_recv()
@@ -748,7 +753,8 @@
             pltpu.VMEM((TM, 16, UNITS_DEV), F32),
             pltpu.VMEM((TM, STIM, TILE), F32),
             pltpu.VMEM((TM, STIM, TILE), F32),
-            pltpu.VMEM((2, SIDE, TILES_DEV // 2, share, FAN * TILE), F32),
+            pltpu.VMEM((2, SIDE, TILES_DEV // 2, share, FAN * TILE), BF16),
+            pltpu.VMEM((2, SIDE, TILES_DEV // 2, share, FAN * TILE), BF16),
             pltpu.VMEM((2, SIDE, TILES_DEV // 2, share, FAN * TILE), BF16),
             pltpu.VMEM((2, TILES_DEV // 2, share, FAN * TILE), BF16),
             pltpu.VMEM((2, 2, TILES_DEV // 2, share, FAN * TILE), BF16),

time: 106 us -> 106 us (level)
  no operation moved by 1% of the time
where the time goes in v8:
time: 106 us
  Pallas kernels  105 us (99%)
    pallas_call x1, Pallas kernels, shards(): pl.pallas_call(main_kernel, out_shape=[pltpu.VMEM((16, UNITS_DEV), F32),...  104 us

profile of v8, /device:TPU:1, one launch (start us, length us, event | category | flops | bytes accessed | tf_op | source)
XLA Modules:
  0.0 105.5 jit_solution(5853260465966959385)
XLA Ops:
  0.6 104.1 %shard_map.120 = (f32[16,1024]{1,0:T(8,128)S(1)}, f32[64,128]{1,0:T(8,128)S(1)}, f32[8,16,512]{2,1,0:T(8,128)S(1)}) custom-call(s32[4,8]{1,0:T(4,128)} %bitcast.11, f32[10]{0:T(128)} %mix.1, s32[512,1024]{1,0:T(8,128)} %spikes_hbm.1, bf16[64,512]{1,0:T(8,128)(2,1)} %bitcast.9, f32[1,1024]{1,0:T(1,128)} %bitcast.10, f32[10,1024]{1,0:T(8,128)} %hist_weight_hbm.1, ...), custom_call_target="tpu_custom_call" | custom-call | tf_op jit(solution)/shard_map/pallas_call | solution.py:717
  104.8 0.8 shard_map.121
